TPU v7x, 32 devices: a whole 2x2x4 slice. The times are simulated.
32 devices in a mesh: node: 4 (over y, core), cores: 8 (over z, x).
Axes of the slice: x: 2, y: 2, z: 4, core: 2. Of those that a mesh axis runs over, the one named last changes fastest.
Arguments:
- fitted: bfloat16 [16, 256, 256, 256], P(None, ('node', 'cores')), may hold values from -0.09375 to 0.09375
- fit_mask: int32 [16, 32], replicated, may hold values 0 or 1
- tasks: int32 [16, 2], replicated, may hold values from 0 to 15, as said below
- owner_map: int32 [16], replicated, may hold values from 0 to 15, each once
- partner: int32 [4], replicated, may hold values from 0 to 3, as said below
- amplitudes: float32 [16, 4, 256, 256], P('cores', None, 'node'), may hold values from -6 to 6
- pair_energy: float32 [4], replicated, may hold values from -1.2 to -0.6
- virt_energy: float32 [1024], replicated, may hold values from 0.1 to 1.2
Outputs:
- new_amplitudes: float32 [16, 4, 256, 256], P('cores', None, 'node')
Inputs may be any that keep to these rules, and one draw needn't show every extreme that they name: `tasks`: each row names an output tile pair and an input tile pair, both numbered X * 4 + Y; no two rows are equal. `owner_map`: each tile pair appears once. partner[partner[p]] = p and partner[p] != p.
All inputs are finite; a program needn't handle non-finite values.
Results may differ from a plain program's by a relative error of at most 0.00057.
Values may be sent and summed in bfloat16 or wider, within the bound.
No kernel may reach another device: no remote copies, remote signals or barrier semaphores. Data moves between devices by JAX's collectives and lax.ppermute only.
A program may use at most 192 MiB of HBM per device.

v0:
```python
import functools
import math

import jax
import jax.numpy as jnp
from jax import lax
from jax.experimental import pallas as pl
from jax.experimental.pallas import tpu as pltpu
from jax.sharding import PartitionSpec as P

AXES = ("node", "cores")


def ladder_kernel(dims, mask_ref, tasks_ref, owner_ref, fitted_ref, *refs):
    nodes, cores, slots_here, rows, tile, aux, slots, side = dims
    amps_refs, refs = refs[:-11], refs[-11:]
    keep_ref, send_ref, left_buf, right_buf, half_buf, tile_buf, total, work, slot_of, load_sems, store_sems = refs
    task_count = tasks_ref.shape[0]
    node_index = lax.axis_index("node")
    core_index = lax.axis_index("cores")
    block = node_index * cores + core_index

    def invert(s, carry):
        slot_of[owner_ref[s]] = s
        return carry

    lax.fori_loop(0, slots, invert, 0)

    def indices(t):
        out_tile = tasks_ref[t, 0]
        in_tile = tasks_ref[t, 1]
        a, b = out_tile // side, out_tile % side
        c, d = in_tile // side, in_tile % side
        return a, b, a * side + c, b * side + d, in_tile

    def enlist(t, count):
        _, _, left, right, _ = indices(t)
        work[count] = t
        return count + mask_ref[left, block] * mask_ref[right, block]

    active = lax.fori_loop(0, task_count, enlist, jnp.int32(0))

    def start_loads(i, slot):
        _, _, left, right, in_tile = indices(work[i])
        place = slot_of[in_tile]
        inside = place % slots_here
        owner = place // slots_here
        apart = owner ^ core_index
        low, far = apart % 2, apart // 2

        def fetch(source, role, node):
            strip = pl.ds(pl.multiple_of(node * rows, rows), rows)
            pltpu.make_async_copy(source, tile_buf.at[slot, role, strip, :], load_sems.at[slot, 2]).start()

        if len(amps_refs) == 1:
            for node in range(nodes):
                fetch(amps_refs[0].at[node * cores + owner, :, inside], slice(None), node)
        else:
            first_refs, second_refs = amps_refs[:nodes], amps_refs[nodes:]
            for other in range(nodes):
                fetch(first_refs[other].at[low, far, inside], 0, node_index ^ other)
            for x in range(2):

                @pl.when(low == x)
                def _():
                    for other in range(nodes):
                        source = second_refs[(other % 2) * 2 + x].at[other // 2, far, inside]
                        fetch(source, 1, node_index ^ other)

        pltpu.make_async_copy(fitted_ref.at[left], left_buf.at[slot], load_sems.at[slot, 0]).start()
        for q in range(aux):
            pltpu.make_async_copy(
                fitted_ref.at[right, q], right_buf.at[slot, :, pl.ds(q * tile, tile)], load_sems.at[slot, 1]
            ).start()

    def wait_loads(slot):
        for k, buf in enumerate((left_buf, right_buf, tile_buf)):
            pltpu.make_async_copy(buf.at[slot], buf.at[slot], load_sems.at[slot, k]).wait()

    @pl.when(active > 0)
    def _():
        start_loads(0, 0)

    @pl.loop(0, slots)
    def _(s):
        total[s] = jnp.zeros(total.shape[1:], jnp.float32)

    def contract(first, second):
        return lax.dot_general(first, second, (((1,), (1,)), ((), ())), preferred_element_type=jnp.float32)

    @pl.loop(0, active)
    def _(i):
        slot = i % 2

        @pl.when(i + 1 < active)
        def _():
            start_loads(i + 1, 1 - slot)

        wait_loads(slot)
        a, b, _, _, _ = indices(work[i])
        straight = slot_of[a * side + b]
        crossed = slot_of[b * side + a]
        left_all = left_buf[slot].reshape(aux * tile, tile)
        for p in range(2):
            half = jnp.dot(left_all, tile_buf[slot, p], preferred_element_type=jnp.float32).astype(jnp.bfloat16)
            for q in range(aux):
                half_buf[p, :, q * tile:(q + 1) * tile] = half[q * tile:(q + 1) * tile]
        shape = total.shape[1:]
        total[straight] += contract(half_buf[0], right_buf[slot]).reshape(shape)
        total[crossed] += contract(right_buf[slot], half_buf[1]).reshape(shape)

    mine = node_index % 2
    stores = [
        pltpu.make_async_copy(total.at[:, :, mine], keep_ref, store_sems.at[0]),
        pltpu.make_async_copy(total.at[:, :, 1 - mine], send_ref, store_sems.at[1]),
    ]
    for copy in stores:
        copy.start()
    for copy in stores:
        copy.wait()


def ladder_terms(mask, tasks, owner_map, fitted, amps, nodes, cores):
    tile_pairs, aux, tile, _ = fitted.shape
    slots_here, rows = tile_pairs // cores, tile // nodes
    side = math.isqrt(tile_pairs)
    dims = (nodes, cores, slots_here, rows, tile, aux, tile_pairs, side)
    smem = pl.BlockSpec(memory_space=pltpu.SMEM)
    hbm = pl.BlockSpec(memory_space=pl.ANY)
    part = jax.ShapeDtypeStruct((tile_pairs, nodes // 2, rows, tile), jnp.float32)
    return pl.pallas_call(
        functools.partial(ladder_kernel, dims),
        out_shape=(part, part),
        in_specs=[smem, smem, smem] + [hbm] * (1 + len(amps)),
        out_specs=(hbm, hbm),
        scratch_shapes=[
            pltpu.VMEM((2, aux, tile, tile), jnp.bfloat16),
            pltpu.VMEM((2, tile, aux * tile), jnp.bfloat16),
            pltpu.VMEM((2, tile, aux * tile), jnp.bfloat16),
            pltpu.VMEM((2, 2, tile, tile), jnp.bfloat16),
            pltpu.VMEM((tile_pairs, nodes // 2, 2, rows, tile), jnp.float32),
            pltpu.SMEM((tasks.shape[0] + 1,), jnp.int32),
            pltpu.SMEM((tile_pairs,), jnp.int32),
            pltpu.SemaphoreType.DMA((2, 3)),
            pltpu.SemaphoreType.DMA((2,)),
        ],
        compiler_params=pltpu.CompilerParams(vmem_limit_bytes=58 * 1024 * 1024),
        cost_estimate=pl.CostEstimate(flops=20 * 10**9, bytes_accessed=30 * 2**20, transcendentals=0),
        name="ladder",
    )(mask, tasks, owner_map, fitted, *amps)


def swap(array, mask, total):
    return lax.ppermute(array, AXES, [(i, i ^ mask) for i in range(total)])


def pick(array, index, axis):
    return lax.dynamic_index_in_dim(array, index, axis, keepdims=False)


def halve(value, index, axis, mask, total):
    shape = value.shape
    split = value.reshape(shape[:axis] + (shape[axis] // 2, 2) + shape[axis + 1:])
    other = swap(pick(split, 1 - index, axis + 1), mask, total)
    own = pick(split, index, axis + 1)
    return (own.astype(jnp.float32) + other.astype(jnp.float32)).astype(value.dtype)


def add_other_core(keep, send, nodes, cores, scale):
    got = swap(send, cores, nodes * cores)
    slots, inner, rows, tile = keep.shape
    part = ((keep + got) * scale).astype(jnp.float16).reshape(cores, slots // cores, inner, rows, tile)
    return part[:, :, :, :rows // 2], part[:, :, :, rows // 2:]


def over_inner(value, nodes, cores):
    mask, index = 2 * cores, lax.axis_index("node") // 2
    while value.shape[2] > 1:
        value = halve(value, index % 2, 2, mask, nodes * cores)
        mask, index = mask * 2, index // 2
    return value


def over_low(value, nodes, cores):
    return halve(value, lax.axis_index("cores") % 2, 0, 1, nodes * cores)


def over_far(upper, lower, nodes, cores, scale):
    part = jnp.concatenate([upper, lower], axis=3)[:, :, 0]
    at = lax.axis_index("cores") // 2
    mine = pick(part, at, 0).astype(jnp.float32)
    for step in range(1, part.shape[0]):
        mine = mine + swap(pick(part, at ^ step, 0), 2 * step, nodes * cores).astype(jnp.float32)
    return mine * (0.5 / scale)


def pair_groups(partner_ref, pairs):
    count = jnp.int32(0)
    chosen = [jnp.int32(0)] * (pairs // 2)
    for p in range(pairs):
        is_rep = p < partner_ref[p]
        chosen = [jnp.where(is_rep & (count == g), p, old) for g, old in enumerate(chosen)]
        count = count + is_rep.astype(jnp.int32)
    return [(p, partner_ref[p]) for p in chosen]


def lower_kernel(partner_ref, amps_ref, *out_refs):
    for out_ref, both in zip(out_refs, pair_groups(partner_ref, amps_ref.shape[1])):
        for role, p in enumerate(both):
            out_ref[role] = amps_ref[:, p].astype(jnp.bfloat16)


def lower(partner, amplitudes):
    slots_here, pairs, rows, tile = amplitudes.shape
    vmem = pl.BlockSpec(memory_space=pltpu.VMEM)
    return pl.pallas_call(
        lower_kernel,
        out_shape=(jax.ShapeDtypeStruct((2, slots_here, rows, tile), jnp.bfloat16),) * (pairs // 2),
        in_specs=[pl.BlockSpec(memory_space=pltpu.SMEM), vmem],
        out_specs=(vmem,) * (pairs // 2),
        name="lower",
    )(partner, amplitudes)


def spread_far(part, cores, total):
    return [part] + [swap(part, 2 * step, total) for step in range(1, cores // 2)]


def spread_inner(parts, nodes, cores):
    total = nodes * cores
    first = jnp.stack([part[0] for part in parts])
    first = jnp.stack([first, swap(first, 1, total)])
    pieces = {0: jnp.stack([part[1] for part in parts])}
    bit = nodes // 2
    while bit > 1:
        pieces.update({other | bit: swap(piece, bit * cores, total) for other, piece in pieces.items()})
        bit //= 2
    return first, jnp.stack([pieces[2 * upper] for upper in range(nodes // 2)])


def spread_outer(first, second, nodes, cores):
    total = nodes * cores
    pieces = {0: first}
    bit = nodes // 2
    while bit > 1:
        pieces.update({other | bit: swap(piece, bit * cores, total) for other, piece in pieces.items()})
        bit //= 2
    return [pieces[2 * upper] for upper in range(1, nodes // 2)], swap(second, 1, total)


def spread_last(first, second, nodes, cores):
    total = nodes * cores
    return [swap(piece, cores, total) for piece in first], [swap(piece, cores, total) for piece in second]


def turn_blocks(mine, nodes, cores, scale):
    total = nodes * cores
    slots_here, rows, tile = mine.shape
    node_index = lax.axis_index("node")
    turned = (mine * scale).astype(jnp.float16).reshape(slots_here * rows, tile).T
    turned = turned.reshape(nodes, rows, slots_here * rows)
    pieces = [pick(turned, node_index, 0)]
    pieces += [swap(pick(turned, node_index ^ step, 0), step * cores, total) for step in range(1, nodes)]
    pieces = jnp.stack(pieces)
    block = jnp.stack([pick(pieces, node_index ^ n, 0) for n in range(nodes)])
    return block.reshape(nodes, rows, slots_here, rows).transpose(2, 1, 0, 3).reshape(slots_here, rows, tile)


def every_block(near, nodes, cores, scale):
    every = jnp.stack([near, swap(near, 1, nodes * cores)], axis=1)
    return every.reshape((cores,) + near.shape[1:]).astype(jnp.float32) * (1.0 / scale)


def update_kernel(side, owner_ref, partner_ref, pair_ref, energy_ref, column_ref, amps_ref, *refs):
    slots_here, pairs, rows, tile = amps_ref.shape
    groups = pairs // 2
    straight, crossed, out_ref, slot_of = refs[:groups], refs[groups:2 * groups], refs[-2], refs[-1]
    node_index = lax.axis_index("node")
    core_index = lax.axis_index("cores")

    def invert(s, carry):
        slot_of[owner_ref[s]] = s
        return carry

    lax.fori_loop(0, owner_ref.shape[0], invert, 0)
    for j in range(slots_here):
        mine = owner_ref[core_index * slots_here + j]
        row_tile, col_tile = mine // side, mine % side
        place = slot_of[col_tile * side + row_tile]
        apart, inside = (place // slots_here) ^ core_index, place % slots_here
        row_energy = energy_ref[pl.ds(pl.multiple_of(row_tile * tile + node_index * rows, 8), rows), :]
        col_energy = column_ref[pl.ds(col_tile, 1), :]
        for g, (rep, twin) in enumerate(pair_groups(partner_ref, pairs)):
            for p, value in ((rep, straight[g][j]), (twin, crossed[g][apart, inside])):
                denominator = (pair_ref[p] - row_energy) - col_energy
                out_ref[j, p] = amps_ref[j, p] + value / denominator


def update(owner_map, partner, pair_energy, virt_energy, amplitudes, straight, crossed):
    tile = amplitudes.shape[3]
    smem = pl.BlockSpec(memory_space=pltpu.SMEM)
    vmem = pl.BlockSpec(memory_space=pltpu.VMEM)
    return pl.pallas_call(
        functools.partial(update_kernel, math.isqrt(owner_map.shape[0])),
        out_shape=jax.ShapeDtypeStruct(amplitudes.shape, jnp.float32),
        in_specs=[smem] * 3 + [vmem] * (3 + len(straight) + len(crossed)),
        out_specs=vmem,
        scratch_shapes=[pltpu.SMEM(owner_map.shape, jnp.int32)],
        compiler_params=pltpu.CompilerParams(vmem_limit_bytes=32 * 1024 * 1024),
        name="update",
    )(
        owner_map, partner, pair_energy, virt_energy.reshape(-1, 1), virt_energy.reshape(-1, tile),
        amplitudes, *straight, *crossed,
    )


def body(nodes, cores, fitted, fit_mask, tasks, owner_map, partner, amplitudes, pair_energy, virt_energy):
    scale = 2.0 ** -9
    total = nodes * cores
    parts = lower(partner, amplitudes)
    groups = len(parts)
    barrier = lax.optimization_barrier

    amps = []
    for g in range(groups - 1):
        inner = spread_inner(spread_far(parts[g], cores, total), nodes, cores)
        outer = spread_outer(*inner, nodes, cores)
        first = [inner[0]] + outer[0]
        second = [inner[1], outer[1]]
        first_far, second_far = spread_last(first, second, nodes, cores)
        amps.append([piece for pair in zip(first, first_far) for piece in pair] + second + second_far)
    amps.append([lax.all_gather(parts[-1], AXES, axis=0, tiled=False)])
    sums = []
    for g in range(groups):
        sums.append(ladder_terms(fit_mask, tasks, owner_map, fitted, amps[g], nodes, cores))
    stages = [
        lambda v: add_other_core(*v, nodes, cores, scale),
        lambda v: barrier((over_inner(v[0], nodes, cores), over_low(v[1], nodes, cores))),
        lambda v: barrier((over_low(v[0], nodes, cores), over_inner(v[1], nodes, cores))),
        lambda v: over_far(*v, nodes, cores, scale),
        lambda v: turn_blocks(v, nodes, cores, scale),
        lambda v: jnp.stack(spread_far(v, cores, total)),
        lambda v: every_block(v, nodes, cores, scale),
    ]
    results = []
    for g in range(groups):
        results.append([sums[g]])
    for step in range(len(stages) + groups - 1):
        for g in reversed(range(groups)):
            stage = step - g
            if not 0 <= stage < len(stages):
                continue
            value = results[g][stage]
            if stage and g + 1 < groups and len(results[g + 1]) > 1:
                value = barrier((value, results[g + 1][-1]))[0]
            results[g].append(stages[stage](value))
    straight = [values[4] for values in results]
    crossed = [values[-1] for values in results]
    return update(owner_map, partner, pair_energy, virt_energy, amplitudes, straight, crossed)


def solution(mesh):
    placed = (P(None, AXES, None, None), P(), P(), P(), P(), P("cores", None, "node", None), P(), P())
    return jax.shard_map(
        functools.partial(body, mesh.shape["node"], mesh.shape["cores"]),
        mesh=mesh, in_specs=placed, out_specs=P("cores", None, "node", None), check_vma=False,
    )
```

profile of v0, /device:TPU:16, one launch (start us, length us, event | category | flops | bytes accessed | tf_op | source)
XLA Modules:
  0.0 183.1 jit_solution(12540911040332276508)
XLA Ops:
  6.5 1.8 lower.1
  8.3 1.6 collective-permute-start
  12.8 2.2 %collective-permute-done = bf16[2,2,64,256]{3,2,1,0:T(8,128)(2,1)S(1)} collective-permute-done((bf16[2,2,64,256]{3,2,1,0:T(8,128)(2,1)}, bf16[2,2,64,256]{3,2,1,0:T(8,128)(2,1)S(1)}, u32[]{:S(2)}, u32[]{:S(2)}) %collective-permute-start) | collective-permute-done | bytes 131104 | tf_op jit(solution)/shard_map/ppermute | solution.py:154
  15.0 5.2 %collective-permute-done.1 = bf16[2,2,64,256]{3,2,1,0:T(8,128)(2,1)S(1)} collective-permute-done((bf16[2,2,64,256]{3,2,1,0:T(8,128)(2,1)}, bf16[2,2,64,256]{3,2,1,0:T(8,128)(2,1)S(1)}, u32[]{:S(2)}, u32[]{:S(2)}) %collective-permute-start.1) | collective-permute-done | bytes 131104 | tf_op jit(solution)/shard_map/ppermute | solution.py:154
  20.2 4.2 %collective-permute-done.2 = bf16[2,2,64,256]{3,2,1,0:T(8,128)(2,1)S(1)} collective-permute-done((bf16[2,2,64,256]{3,2,1,0:T(8,128)(2,1)}, bf16[2,2,64,256]{3,2,1,0:T(8,128)(2,1)S(1)}, u32[]{:S(2)}, u32[]{:S(2)}) %collective-permute-start.2) | collective-permute-done | bytes 131104 | tf_op jit(solution)/shard_map/ppermute | solution.py:154
  27.7 4.0 %collective-permute-done.7 = bf16[4,2,64,256]{3,2,1,0:T(8,128)(2,1)S(1)} collective-permute-done((bf16[4,2,64,256]{3,2,1,0:T(8,128)(2,1)S(1)}, bf16[4,2,64,256]{3,2,1,0:T(8,128)(2,1)S(1)}, u32[]{:S(2)}, u32[]{:S(2)}) %collective-permute-start.7) | collective-permute-done | bytes 262176 | tf_op jit(solution)/shard_map/ppermute | solution.py:154
  35.4 12.5 %collective-permute-done.8.refs_5_ = bf16[2,4,2,64,256]{4,3,2,1,0:T(8,128)(2,1)S(1)} collective-permute-done((bf16[2,4,2,64,256]{4,3,2,1,0:T(8,128)(2,1)S(1)}, bf16[2,4,2,64,256]{4,3,2,1,0:T(8,128)(2,1)S(1)}, u32[]{:S(2)}, u32[]{:S(2)}) %collective-permute-start.8) | collective-permute-done | bytes 524320 | tf_op jit(solution)/shard_map/ppermute | solution.py:154
  50.7 18.6 %ladder.2 = (f32[16,2,64,256]{3,2,1,0:T(8,128)}, f32[16,2,64,256]{3,2,1,0:T(8,128)}) custom-call(s32[16,32]{1,0:T(8,128)} %mask_ref.3, s32[16,2]{1,0:T(8,128)} %copy.42.tasks_ref, s32[16]{0:T(128)} %owner_ref.5, bf16[16,8,256,256]{3,2,1,0:T(8,128)(2,1)} %fitted_ref.3, bf16[2,4,2,64,256]{4,3,2,1,0:T(8,128)(2,1)} %copy-done.7, ...), custom_call_target="tpu_custom_call" | custom-call | flops 20000000000 | bytes 31457280 | tf_op jit(solution)/shard_map/ladder/pallas_call | solution.py:131
  69.4 5.3 %all-gather.3.cloned.1.call-done = bf16[64,2,64,256]{3,2,1,0:T(8,128)(2,1)} async-done(((bf16[2,2,64,256]{3,2,1,0:T(8,128)(2,1)}), bf16[64,2,64,256]{3,2,1,0:T(8,128)(2,1)}) %all-gather.3.cloned.1.call-update) | async-done | bytes 4194320 | tf_op jit(solution)/shard_map/all_gather | solution.py:332
  74.7 18.3 %ladder.3 = (f32[16,2,64,256]{3,2,1,0:T(8,128)}, f32[16,2,64,256]{3,2,1,0:T(8,128)}) custom-call(s32[16,32]{1,0:T(8,128)} %mask_ref.3, s32[16,2]{1,0:T(8,128)} %copy.42.tasks_ref, s32[16]{0:T(128)} %owner_ref.5, bf16[16,8,256,256]{3,2,1,0:T(8,128)(2,1)} %fitted_ref.3, bf16[32,2,2,64,256]{4,3,2,1,0:T(8,128)(2,1)} %bitcast.145), custom_call_target="tpu_custom_call" | custom-call | flops 20000000000 | bytes 31457280 | tf_op jit(solution)/shard_map/ladder/pallas_call | solution.py:131
  93.2 2.2 %multiply_convert_fusion.1 = f16[16,2,64,256]{3,2,1,0:T(8,128)(2,1)S(1)} fusion(f32[16,2,64,256]{3,2,1,0:T(8,128)S(1)} %copy-done.4, f32[16,2,64,256]{3,2,1,0:T(8,128)} %collective-permute-done.11), kind=kLoop, calls=%fused_computation.1 | loop fusion | flops 1572864 | bytes 5242880 | tf_op jit(solution)/shard_map/convert_element_type | solution.py:172
  95.4 2.1 %collective-permute-done.12 = f32[16,2,64,256]{3,2,1,0:T(8,128)} collective-permute-done((f32[16,2,64,256]{3,2,1,0:T(8,128)}, f32[16,2,64,256]{3,2,1,0:T(8,128)}, u32[]{:S(2)}, u32[]{:S(2)}) %collective-permute-start.12) | collective-permute-done | bytes 2097184 | tf_op jit(solution)/shard_map/ppermute | solution.py:154
  97.6 2.1 %multiply_convert_fusion = f16[16,2,64,256]{3,2,1,0:T(8,128)(2,1)S(1)} fusion(f32[16,2,64,256]{3,2,1,0:T(8,128)S(1)} %copy-done.5, f32[16,2,64,256]{3,2,1,0:T(8,128)} %collective-permute-done.12), kind=kLoop, calls=%fused_computation | loop fusion | flops 1572864 | bytes 5242880 | tf_op jit(solution)/shard_map/convert_element_type | solution.py:172
  100.6 1.6 collective-permute-start.16
  102.3 12.1 %collective-permute-start.15 = (f16[8,2,1,32,256]{4,3,2,1,0:T(8,128)(2,1)S(1)}, f16[8,2,1,32,256]{4,3,2,1,0:T(8,128)(2,1)S(1)}, u32[]{:S(2)}, u32[]{:S(2)}) collective-permute-start(f16[8,2,1,32,256]{4,3,2,1,0:T(8,128)(2,1)S(1)} %constant_dynamic-slice_fusion.14), channel_id=1, source_target_pairs={{0,16},{1,17},{2,18},{3,19},{4,20},{5,21},{6,22},{7,23},{8,24},{9,... | collective-permute-start | bytes 786440 | tf_op jit(solution)/shard_map/ppermute | solution.py:154
  114.6 2.1 %collective-permute-start.14 = (f16[4,2,2,32,256]{4,3,1,2,0:T(8,128)(2,1)S(1)}, f16[4,2,2,32,256]{4,3,1,2,0:T(8,128)(2,1)S(1)}, u32[]{:S(2)}, u32[]{:S(2)}) collective-permute-start(f16[4,2,2,32,256]{4,3,1,2,0:T(8,128)(2,1)S(1)} %bitcast.122), channel_id=1, source_target_pairs={{0,1},{1,0},{2,3},{3,2},{4,5},{5,4},{6,7},{7,6},{8,9},{9,8},{10,11... | collective-permute-start | bytes 786440 | tf_op jit(solution)/shard_map/ppermute | solution.py:154
  116.9 4.6 %collective-permute-done.15 = f16[8,2,1,32,256]{4,3,2,1,0:T(8,128)(2,1)S(1)} collective-permute-done((f16[8,2,1,32,256]{4,3,2,1,0:T(8,128)(2,1)S(1)}, f16[8,2,1,32,256]{4,3,2,1,0:T(8,128)(2,1)S(1)}, u32[]{:S(2)}, u32[]{:S(2)}) %collective-permute-start.15) | collective-permute-done | bytes 262176 | tf_op jit(solution)/shard_map/ppermute | solution.py:154
  121.6 2.1 %collective-permute-start.20 = (f16[4,2,1,32,256]{4,3,1,2,0:T(8,128)(2,1)S(1)}, f16[4,2,1,32,256]{4,3,1,2,0:T(8,128)(2,1)S(1)}, u32[]{:S(2)}, u32[]{:S(2)}) collective-permute-start(f16[4,2,1,32,256]{4,3,1,2,0:T(8,128)(2,1)S(1)} %constant_dynamic-slice_fusion.10), channel_id=1, source_target_pairs={{0,16},{1,17},{2,18},{3,19},{4,20},{5,21},{6,22},{7,23},{8,24},{9,... | collective-permute-start | bytes 393224 | tf_op jit(solution)/shard_map/ppermute | solution.py:154
  123.8 2.1 %collective-permute-start.19 = (f16[4,2,1,32,256]{4,3,1,2,0:T(8,128)(2,1)S(1)}, f16[4,2,1,32,256]{4,3,1,2,0:T(8,128)(2,1)S(1)}, u32[]{:S(2)}, u32[]{:S(2)}) collective-permute-start(f16[4,2,1,32,256]{4,3,1,2,0:T(8,128)(2,1)S(1)} %dynamic-slice_bitcast_fusion), channel_id=1, source_target_pairs={{0,1},{1,0},{2,3},{3,2},{4,5},{5,4},{6,7},{7,6},{8,9},{9,8},{10,11... | collective-permute-start | bytes 393224 | tf_op jit(solution)/shard_map/ppermute | solution.py:154
  127.3 2.1 %collective-permute-start.18 = (f16[4,2,1,32,256]{4,3,1,2,0:T(8,128)(2,1)S(1)}, f16[4,2,1,32,256]{4,3,1,2,0:T(8,128)(2,1)S(1)}, u32[]{:S(2)}, u32[]{:S(2)}) collective-permute-start(f16[4,2,1,32,256]{4,3,1,2,0:T(8,128)(2,1)S(1)} %constant_dynamic-slice_fusion.11), channel_id=1, source_target_pairs={{0,16},{1,17},{2,18},{3,19},{4,20},{5,21},{6,22},{7,23},{8,24},{9,... | collective-permute-start | bytes 393224 | tf_op jit(solution)/shard_map/ppermute | solution.py:154
  129.5 2.1 %collective-permute-start.17 = (f16[4,2,1,32,256]{4,3,1,2,0:T(8,128)(2,1)S(1)}, f16[4,2,1,32,256]{4,3,1,2,0:T(8,128)(2,1)S(1)}, u32[]{:S(2)}, u32[]{:S(2)}) collective-permute-start(f16[4,2,1,32,256]{4,3,1,2,0:T(8,128)(2,1)S(1)} %dynamic-slice_bitcast_fusion.1), channel_id=1, source_target_pairs={{0,1},{1,0},{2,3},{3,2},{4,5},{5,4},{6,7},{7,6},{8,9},{9,8},{10,11... | collective-permute-start | bytes 393224 | tf_op jit(solution)/shard_map/ppermute | solution.py:154
  132.0 3.4 %collective-permute-start.26 = (f16[2,64,256]{2,1,0:T(8,128)(2,1)S(1)}, f16[2,64,256]{2,1,0:T(8,128)(2,1)S(1)}, u32[]{:S(2)}, u32[]{:S(2)}) collective-permute-start(f16[2,64,256]{2,1,0:T(8,128)(2,1)S(1)} %get-tuple-element.64), channel_id=1, source_target_pairs={{0,6},{1,7},{2,4},{3,5},{4,2},{5,3},{6,0},{7,1},{8,14},{9,15},{10,... | collective-permute-start | bytes 196616 | tf_op jit(solution)/shard_map/ppermute | solution.py:154
  137.2 2.0 %collective-permute-start.23 = (f16[2,64,256]{2,1,0:T(8,128)(2,1)S(1)}, f16[2,64,256]{2,1,0:T(8,128)(2,1)S(1)}, u32[]{:S(2)}, u32[]{:S(2)}) collective-permute-start(f16[2,64,256]{2,1,0:T(8,128)(2,1)S(1)} %get-tuple-element.67), channel_id=1, source_target_pairs={{0,6},{1,7},{2,4},{3,5},{4,2},{5,3},{6,0},{7,1},{8,14},{9,15},{10,... | collective-permute-start | bytes 196616 | tf_op jit(solution)/shard_map/ppermute | solution.py:154
  139.2 3.2 %collective-permute-done.26 = f16[2,64,256]{2,1,0:T(8,128)(2,1)S(1)} collective-permute-done((f16[2,64,256]{2,1,0:T(8,128)(2,1)S(1)}, f16[2,64,256]{2,1,0:T(8,128)(2,1)S(1)}, u32[]{:S(2)}, u32[]{:S(2)}) %collective-permute-start.26) | collective-permute-done | bytes 65568 | tf_op jit(solution)/shard_map/ppermute | solution.py:154
  149.5 2.3 %collective-permute-start.38 = (f16[2,64,256]{2,1,0:T(8,128)(2,1)S(1)}, f16[2,64,256]{2,1,0:T(8,128)(2,1)S(1)}, u32[]{:S(2)}, u32[]{:S(2)}) collective-permute-start(f16[2,64,256]{2,1,0:T(8,128)(2,1)S(1)} %reshape.151), channel_id=1, source_target_pairs={{0,6},{1,7},{2,4},{3,5},{4,2},{5,3},{6,0},{7,1},{8,14},{9,15},{10,... | collective-permute-start | bytes 196616 | tf_op jit(solution)/shard_map/ppermute | solution.py:154
  153.8 2.0 %collective-permute-start.35 = (f16[2,64,256]{2,1,0:T(8,128)(2,1)S(1)}, f16[2,64,256]{2,1,0:T(8,128)(2,1)S(1)}, u32[]{:S(2)}, u32[]{:S(2)}) collective-permute-start(f16[2,64,256]{2,1,0:T(8,128)(2,1)S(1)} %reshape.147), channel_id=1, source_target_pairs={{0,6},{1,7},{2,4},{3,5},{4,2},{5,3},{6,0},{7,1},{8,14},{9,15},{10,... | collective-permute-start | bytes 196616 | tf_op jit(solution)/shard_map/ppermute | solution.py:154
  155.8 3.8 %collective-permute-done.38 = f16[2,64,256]{2,1,0:T(8,128)(2,1)S(1)} collective-permute-done((f16[2,64,256]{2,1,0:T(8,128)(2,1)S(1)}, f16[2,64,256]{2,1,0:T(8,128)(2,1)S(1)}, u32[]{:S(2)}, u32[]{:S(2)}) %collective-permute-start.38) | collective-permute-done | bytes 65568 | tf_op jit(solution)/shard_map/ppermute | solution.py:154
  159.7 2.6 %collective-permute-start.40 = (f16[4,2,64,256]{3,2,1,0:T(8,128)(2,1)S(1)}, f16[4,2,64,256]{3,2,1,0:T(8,128)(2,1)S(1)}, u32[]{:S(2)}, u32[]{:S(2)}) collective-permute-start(f16[4,2,64,256]{3,2,1,0:T(8,128)(2,1)S(1)} %get-tuple-element.62), channel_id=1, source_target_pairs={{0,1},{1,0},{2,3},{3,2},{4,5},{5,4},{6,7},{7,6},{8,9},{9,8},{10,11... | collective-permute-start | bytes 786440 | tf_op jit(solution)/shard_map/ppermute | solution.py:154
  163.1 1.9 %collective-permute-start.39 = (f16[4,2,64,256]{3,2,1,0:T(8,128)(2,1)S(1)}, f16[4,2,64,256]{3,2,1,0:T(8,128)(2,1)S(1)}, u32[]{:S(2)}, u32[]{:S(2)}) collective-permute-start(f16[4,2,64,256]{3,2,1,0:T(8,128)(2,1)S(1)} %pad_maximum_fusion.4), channel_id=1, source_target_pairs={{0,1},{1,0},{2,3},{3,2},{4,5},{5,4},{6,7},{7,6},{8,9},{9,8},{10,11... | collective-permute-start | bytes 786440 | tf_op jit(solution)/shard_map/ppermute | solution.py:154
  165.2 4.2 %collective-permute-done.40 = f16[4,2,64,256]{3,2,1,0:T(8,128)(2,1)S(1)} collective-permute-done((f16[4,2,64,256]{3,2,1,0:T(8,128)(2,1)S(1)}, f16[4,2,64,256]{3,2,1,0:T(8,128)(2,1)S(1)}, u32[]{:S(2)}, u32[]{:S(2)}) %collective-permute-start.40) | collective-permute-done | bytes 262176 | tf_op jit(solution)/shard_map/ppermute | solution.py:154
  169.7 4.6 %collective-permute-done.39 = f16[4,2,64,256]{3,2,1,0:T(8,128)(2,1)S(1)} collective-permute-done((f16[4,2,64,256]{3,2,1,0:T(8,128)(2,1)S(1)}, f16[4,2,64,256]{3,2,1,0:T(8,128)(2,1)S(1)}, u32[]{:S(2)}, u32[]{:S(2)}) %collective-permute-start.39) | collective-permute-done | bytes 262176 | tf_op jit(solution)/shard_map/ppermute | solution.py:154
  174.6 1.7 update.1
  (149 shorter events, 28.4 us)
Async XLA Ops:
  6.5 68.1 %all-gather.3.cloned.1.call-start = ((), (), s32[]{:S(2)}) async-start(), calls=%async_computation | async-start | bytes 4325376 | tf_op jit(solution)/shard_map/all_gather | solution.py:332
  8.3 6.7 %collective-permute-start = (bf16[2,2,64,256]{3,2,1,0:T(8,128)(2,1)}, bf16[2,2,64,256]{3,2,1,0:T(8,128)(2,1)S(1)}, u32[]{:S(2)}, u32[]{:S(2)}) collective-permute-start(bf16[2,2,64,256]{3,2,1,0:T(8,128)(2,1)} %get-tuple-element.28), channel_id=1, source_target_pairs={{0,2},{1,3},{2,0},{3,1},{4,6},{5,7},{6,4},{7,5},{8,10},{9,11},{10,... | collective-permute-start | bytes 393224 | tf_op jit(solution)/shard_map/ppermute | solution.py:154
  10.0 10.2 %collective-permute-start.1 = (bf16[2,2,64,256]{3,2,1,0:T(8,128)(2,1)}, bf16[2,2,64,256]{3,2,1,0:T(8,128)(2,1)S(1)}, u32[]{:S(2)}, u32[]{:S(2)}) collective-permute-start(bf16[2,2,64,256]{3,2,1,0:T(8,128)(2,1)} %get-tuple-element.28), channel_id=1, source_target_pairs={{0,4},{1,5},{2,6},{3,7},{4,0},{5,1},{6,2},{7,3},{8,12},{9,13},{10,... | collective-permute-start | bytes 393224 | tf_op jit(solution)/shard_map/ppermute | solution.py:154
  10.3 14.1 %collective-permute-start.2 = (bf16[2,2,64,256]{3,2,1,0:T(8,128)(2,1)}, bf16[2,2,64,256]{3,2,1,0:T(8,128)(2,1)S(1)}, u32[]{:S(2)}, u32[]{:S(2)}) collective-permute-start(bf16[2,2,64,256]{3,2,1,0:T(8,128)(2,1)} %get-tuple-element.28), channel_id=1, source_target_pairs={{0,6},{1,7},{2,4},{3,5},{4,2},{5,3},{6,0},{7,1},{8,14},{9,15},{10,... | collective-permute-start | bytes 393224 | tf_op jit(solution)/shard_map/ppermute | solution.py:154
  24.5 7.2 %collective-permute-start.7 = (bf16[4,2,64,256]{3,2,1,0:T(8,128)(2,1)S(1)}, bf16[4,2,64,256]{3,2,1,0:T(8,128)(2,1)S(1)}, u32[]{:S(2)}, u32[]{:S(2)}) collective-permute-start(bf16[4,2,64,256]{3,2,1,0:T(8,128)(2,1)S(1)} %get-tuple-element.70), channel_id=1, source_target_pairs={{0,16},{1,17},{2,18},{3,19},{4,20},{5,21},{6,22},{7,23},{8,24},{9,... | collective-permute-start | bytes 786440 | tf_op jit(solution)/shard_map/ppermute | solution.py:154
  26.1 7.4 %collective-permute-start.3 = (bf16[4,2,64,256]{3,2,1,0:T(8,128)(2,1)S(1)}, bf16[4,2,64,256]{3,2,1,0:T(8,128)(2,1)S(1)}, u32[]{:S(2)}, u32[]{:S(2)}) collective-permute-start(bf16[4,2,64,256]{3,2,1,0:T(8,128)(2,1)S(1)} %get-tuple-element.72), channel_id=1, source_target_pairs={{0,1},{1,0},{2,3},{3,2},{4,5},{5,4},{6,7},{7,6},{8,9},{9,8},{10,11... | collective-permute-start | bytes 786440 | tf_op jit(solution)/shard_map/ppermute | solution.py:154
  31.7 16.1 %collective-permute-start.8 = (bf16[2,4,2,64,256]{4,3,2,1,0:T(8,128)(2,1)S(1)}, bf16[2,4,2,64,256]{4,3,2,1,0:T(8,128)(2,1)S(1)}, u32[]{:S(2)}, u32[]{:S(2)}) collective-permute-start(bf16[2,4,2,64,256]{4,3,2,1,0:T(8,128)(2,1)S(1)} %pad_maximum_fusion.1.refs_4_), channel_id=1, source_target_pairs={{0,1},{1,0},{2,3},{3,2},{4,5},{5,4},{6,7},{7,6},{8,9},{9,8},{10,11... | collective-permute-start | bytes 1572872 | tf_op jit(solution)/shard_map/ppermute | solution.py:154
  33.5 14.3 %collective-permute-start.5 = (bf16[2,4,2,64,256]{4,3,2,1,0:T(8,128)(2,1)S(1)}, bf16[2,4,2,64,256]{4,3,2,1,0:T(8,128)(2,1)S(1)}, u32[]{:S(2)}, u32[]{:S(2)}) collective-permute-start(bf16[2,4,2,64,256]{4,3,2,1,0:T(8,128)(2,1)S(1)} %pad_maximum_fusion.refs_0_), channel_id=1, source_target_pairs={{0,16},{1,17},{2,18},{3,19},{4,20},{5,21},{6,22},{7,23},{8,24},{9,... | collective-permute-start | bytes 1572872 | tf_op jit(solution)/shard_map/ppermute | solution.py:154
  34.9 14.2 %collective-permute-start.4 = (bf16[2,4,2,64,256]{4,3,2,1,0:T(8,128)(2,1)S(1)}, bf16[2,4,2,64,256]{4,3,2,1,0:T(8,128)(2,1)S(1)}, u32[]{:S(2)}, u32[]{:S(2)}) collective-permute-start(bf16[2,4,2,64,256]{4,3,2,1,0:T(8,128)(2,1)S(1)} %pad_maximum_fusion.refs_0_), channel_id=1, source_target_pairs={{0,8},{1,9},{2,10},{3,11},{4,12},{5,13},{6,14},{7,15},{8,0},{9,1},... | collective-permute-start | bytes 1572872 | tf_op jit(solution)/shard_map/ppermute | solution.py:154
  34.9 14.2 %collective-permute-start.9 = (bf16[2,4,2,64,256]{4,3,2,1,0:T(8,128)(2,1)S(1)}, bf16[2,4,2,64,256]{4,3,2,1,0:T(8,128)(2,1)S(1)}, u32[]{:S(2)}, u32[]{:S(2)}) collective-permute-start(bf16[2,4,2,64,256]{4,3,2,1,0:T(8,128)(2,1)S(1)} %pad_maximum_fusion.1.refs_4_), channel_id=1, source_target_pairs={{0,8},{1,9},{2,10},{3,11},{4,12},{5,13},{6,14},{7,15},{8,0},{9,1},... | collective-permute-start | bytes 1572872 | tf_op jit(solution)/shard_map/ppermute | solution.py:154
  69.3 23.9 %collective-permute-start.11 = (f32[16,2,64,256]{3,2,1,0:T(8,128)}, f32[16,2,64,256]{3,2,1,0:T(8,128)}, u32[]{:S(2)}, u32[]{:S(2)}) collective-permute-start(f32[16,2,64,256]{3,2,1,0:T(8,128)} %get-tuple-element.30), channel_id=1, source_target_pairs={{0,8},{1,9},{2,10},{3,11},{4,12},{5,13},{6,14},{7,15},{8,0},{9,1},... | collective-permute-start | bytes 6291464 | tf_op jit(solution)/shard_map/ppermute | solution.py:154
  100.6 16.2 %collective-permute-start.16 = (f16[4,2,2,32,256]{4,3,1,2,0:T(8,128)(2,1)S(1)}, f16[4,2,2,32,256]{4,3,1,2,0:T(8,128)(2,1)S(1)}, u32[]{:S(2)}, u32[]{:S(2)}) collective-permute-start(f16[4,2,2,32,256]{4,3,1,2,0:T(8,128)(2,1)S(1)} %bitcast.123), channel_id=1, source_target_pairs={{0,1},{1,0},{2,3},{3,2},{4,5},{5,4},{6,7},{7,6},{8,9},{9,8},{10,11... | collective-permute-start | bytes 786440 | tf_op jit(solution)/shard_map/ppermute | solution.py:154
  102.3 19.2 %collective-permute-start.15 = (f16[8,2,1,32,256]{4,3,2,1,0:T(8,128)(2,1)S(1)}, f16[8,2,1,32,256]{4,3,2,1,0:T(8,128)(2,1)S(1)}, u32[]{:S(2)}, u32[]{:S(2)}) collective-permute-start(f16[8,2,1,32,256]{4,3,2,1,0:T(8,128)(2,1)S(1)} %constant_dynamic-slice_fusion.14), channel_id=1, source_target_pairs={{0,16},{1,17},{2,18},{3,19},{4,20},{5,21},{6,22},{7,23},{8,24},{9,... | collective-permute-start | bytes 786440 | tf_op jit(solution)/shard_map/ppermute | solution.py:154
  114.6 12.6 %collective-permute-start.14 = (f16[4,2,2,32,256]{4,3,1,2,0:T(8,128)(2,1)S(1)}, f16[4,2,2,32,256]{4,3,1,2,0:T(8,128)(2,1)S(1)}, u32[]{:S(2)}, u32[]{:S(2)}) collective-permute-start(f16[4,2,2,32,256]{4,3,1,2,0:T(8,128)(2,1)S(1)} %bitcast.122), channel_id=1, source_target_pairs={{0,1},{1,0},{2,3},{3,2},{4,5},{5,4},{6,7},{7,6},{8,9},{9,8},{10,11... | collective-permute-start | bytes 786440 | tf_op jit(solution)/shard_map/ppermute | solution.py:154
  116.7 10.4 %collective-permute-start.13 = (f16[8,2,1,32,256]{4,3,2,1,0:T(8,128)(2,1)S(1)}, f16[8,2,1,32,256]{4,3,2,1,0:T(8,128)(2,1)S(1)}, u32[]{:S(2)}, u32[]{:S(2)}) collective-permute-start(f16[8,2,1,32,256]{4,3,2,1,0:T(8,128)(2,1)S(1)} %constant_dynamic-slice_fusion.17), channel_id=1, source_target_pairs={{0,16},{1,17},{2,18},{3,19},{4,20},{5,21},{6,22},{7,23},{8,24},{9,... | collective-permute-start | bytes 786440 | tf_op jit(solution)/shard_map/ppermute | solution.py:154
  121.6 10.0 %collective-permute-start.20 = (f16[4,2,1,32,256]{4,3,1,2,0:T(8,128)(2,1)S(1)}, f16[4,2,1,32,256]{4,3,1,2,0:T(8,128)(2,1)S(1)}, u32[]{:S(2)}, u32[]{:S(2)}) collective-permute-start(f16[4,2,1,32,256]{4,3,1,2,0:T(8,128)(2,1)S(1)} %constant_dynamic-slice_fusion.10), channel_id=1, source_target_pairs={{0,16},{1,17},{2,18},{3,19},{4,20},{5,21},{6,22},{7,23},{8,24},{9,... | collective-permute-start | bytes 393224 | tf_op jit(solution)/shard_map/ppermute | solution.py:154
  123.8 7.9 %collective-permute-start.19 = (f16[4,2,1,32,256]{4,3,1,2,0:T(8,128)(2,1)S(1)}, f16[4,2,1,32,256]{4,3,1,2,0:T(8,128)(2,1)S(1)}, u32[]{:S(2)}, u32[]{:S(2)}) collective-permute-start(f16[4,2,1,32,256]{4,3,1,2,0:T(8,128)(2,1)S(1)} %dynamic-slice_bitcast_fusion), channel_id=1, source_target_pairs={{0,1},{1,0},{2,3},{3,2},{4,5},{5,4},{6,7},{7,6},{8,9},{9,8},{10,11... | collective-permute-start | bytes 393224 | tf_op jit(solution)/shard_map/ppermute | solution.py:154
  127.3 8.1 %collective-permute-start.18 = (f16[4,2,1,32,256]{4,3,1,2,0:T(8,128)(2,1)S(1)}, f16[4,2,1,32,256]{4,3,1,2,0:T(8,128)(2,1)S(1)}, u32[]{:S(2)}, u32[]{:S(2)}) collective-permute-start(f16[4,2,1,32,256]{4,3,1,2,0:T(8,128)(2,1)S(1)} %constant_dynamic-slice_fusion.11), channel_id=1, source_target_pairs={{0,16},{1,17},{2,18},{3,19},{4,20},{5,21},{6,22},{7,23},{8,24},{9,... | collective-permute-start | bytes 393224 | tf_op jit(solution)/shard_map/ppermute | solution.py:154
  129.5 6.0 %collective-permute-start.17 = (f16[4,2,1,32,256]{4,3,1,2,0:T(8,128)(2,1)S(1)}, f16[4,2,1,32,256]{4,3,1,2,0:T(8,128)(2,1)S(1)}, u32[]{:S(2)}, u32[]{:S(2)}) collective-permute-start(f16[4,2,1,32,256]{4,3,1,2,0:T(8,128)(2,1)S(1)} %dynamic-slice_bitcast_fusion.1), channel_id=1, source_target_pairs={{0,1},{1,0},{2,3},{3,2},{4,5},{5,4},{6,7},{7,6},{8,9},{9,8},{10,11... | collective-permute-start | bytes 393224 | tf_op jit(solution)/shard_map/ppermute | solution.py:154
  131.9 7.3 %collective-permute-start.25 = (f16[2,64,256]{2,1,0:T(8,128)(2,1)S(1)}, f16[2,64,256]{2,1,0:T(8,128)(2,1)S(1)}, u32[]{:S(2)}, u32[]{:S(2)}) collective-permute-start(f16[2,64,256]{2,1,0:T(8,128)(2,1)S(1)} %get-tuple-element.65), channel_id=1, source_target_pairs={{0,4},{1,5},{2,6},{3,7},{4,0},{5,1},{6,2},{7,3},{8,12},{9,13},{10,... | collective-permute-start | bytes 196616 | tf_op jit(solution)/shard_map/ppermute | solution.py:154
  132.0 10.4 %collective-permute-start.26 = (f16[2,64,256]{2,1,0:T(8,128)(2,1)S(1)}, f16[2,64,256]{2,1,0:T(8,128)(2,1)S(1)}, u32[]{:S(2)}, u32[]{:S(2)}) collective-permute-start(f16[2,64,256]{2,1,0:T(8,128)(2,1)S(1)} %get-tuple-element.64), channel_id=1, source_target_pairs={{0,6},{1,7},{2,4},{3,5},{4,2},{5,3},{6,0},{7,1},{8,14},{9,15},{10,... | collective-permute-start | bytes 196616 | tf_op jit(solution)/shard_map/ppermute | solution.py:154
  135.7 8.6 %collective-permute-start.21 = (f16[2,64,256]{2,1,0:T(8,128)(2,1)S(1)}, f16[2,64,256]{2,1,0:T(8,128)(2,1)S(1)}, u32[]{:S(2)}, u32[]{:S(2)}) collective-permute-start(f16[2,64,256]{2,1,0:T(8,128)(2,1)S(1)} %get-tuple-element.66), channel_id=1, source_target_pairs={{0,2},{1,3},{2,0},{3,1},{4,6},{5,7},{6,4},{7,5},{8,10},{9,11},{10,... | collective-permute-start | bytes 196616 | tf_op jit(solution)/shard_map/ppermute | solution.py:154
  136.7 7.9 %collective-permute-start.22 = (f16[2,64,256]{2,1,0:T(8,128)(2,1)S(1)}, f16[2,64,256]{2,1,0:T(8,128)(2,1)S(1)}, u32[]{:S(2)}, u32[]{:S(2)}) collective-permute-start(f16[2,64,256]{2,1,0:T(8,128)(2,1)S(1)} %get-tuple-element.68), channel_id=1, source_target_pairs={{0,4},{1,5},{2,6},{3,7},{4,0},{5,1},{6,2},{7,3},{8,12},{9,13},{10,... | collective-permute-start | bytes 196616 | tf_op jit(solution)/shard_map/ppermute | solution.py:154
  137.2 7.4 %collective-permute-start.23 = (f16[2,64,256]{2,1,0:T(8,128)(2,1)S(1)}, f16[2,64,256]{2,1,0:T(8,128)(2,1)S(1)}, u32[]{:S(2)}, u32[]{:S(2)}) collective-permute-start(f16[2,64,256]{2,1,0:T(8,128)(2,1)S(1)} %get-tuple-element.67), channel_id=1, source_target_pairs={{0,6},{1,7},{2,4},{3,5},{4,2},{5,3},{6,0},{7,1},{8,14},{9,15},{10,... | collective-permute-start | bytes 196616 | tf_op jit(solution)/shard_map/ppermute | solution.py:154
  145.2 6.5 %collective-permute-start.28 = (f16[64,128]{1,0:T(8,128)(2,1)S(1)}, f16[64,128]{1,0:T(8,128)(2,1)S(1)}, u32[]{:S(2)}, u32[]{:S(2)}) collective-permute-start(f16[64,128]{1,0:T(8,128)(2,1)S(1)} %get-tuple-element.95), channel_id=1, source_target_pairs={{0,16},{1,17},{2,18},{3,19},{4,20},{5,21},{6,22},{7,23},{8,24},{9,... | collective-permute-start | bytes 49160 | tf_op jit(solution)/shard_map/ppermute | solution.py:154
  148.1 7.8 %collective-permute-start.37 = (f16[2,64,256]{2,1,0:T(8,128)(2,1)S(1)}, f16[2,64,256]{2,1,0:T(8,128)(2,1)S(1)}, u32[]{:S(2)}, u32[]{:S(2)}) collective-permute-start(f16[2,64,256]{2,1,0:T(8,128)(2,1)S(1)} %reshape.151), channel_id=1, source_target_pairs={{0,4},{1,5},{2,6},{3,7},{4,0},{5,1},{6,2},{7,3},{8,12},{9,13},{10,... | collective-permute-start | bytes 196616 | tf_op jit(solution)/shard_map/ppermute | solution.py:154
  149.5 10.1 %collective-permute-start.38 = (f16[2,64,256]{2,1,0:T(8,128)(2,1)S(1)}, f16[2,64,256]{2,1,0:T(8,128)(2,1)S(1)}, u32[]{:S(2)}, u32[]{:S(2)}) collective-permute-start(f16[2,64,256]{2,1,0:T(8,128)(2,1)S(1)} %reshape.151), channel_id=1, source_target_pairs={{0,6},{1,7},{2,4},{3,5},{4,2},{5,3},{6,0},{7,1},{8,14},{9,15},{10,... | collective-permute-start | bytes 196616 | tf_op jit(solution)/shard_map/ppermute | solution.py:154
  152.3 10.0 %collective-permute-start.33 = (f16[2,64,256]{2,1,0:T(8,128)(2,1)S(1)}, f16[2,64,256]{2,1,0:T(8,128)(2,1)S(1)}, u32[]{:S(2)}, u32[]{:S(2)}) collective-permute-start(f16[2,64,256]{2,1,0:T(8,128)(2,1)S(1)} %reshape.147), channel_id=1, source_target_pairs={{0,2},{1,3},{2,0},{3,1},{4,6},{5,7},{6,4},{7,5},{8,10},{9,11},{10,... | collective-permute-start | bytes 196616 | tf_op jit(solution)/shard_map/ppermute | solution.py:154
  153.3 9.0 %collective-permute-start.34 = (f16[2,64,256]{2,1,0:T(8,128)(2,1)S(1)}, f16[2,64,256]{2,1,0:T(8,128)(2,1)S(1)}, u32[]{:S(2)}, u32[]{:S(2)}) collective-permute-start(f16[2,64,256]{2,1,0:T(8,128)(2,1)S(1)} %reshape.147), channel_id=1, source_target_pairs={{0,4},{1,5},{2,6},{3,7},{4,0},{5,1},{6,2},{7,3},{8,12},{9,13},{10,... | collective-permute-start | bytes 196616 | tf_op jit(solution)/shard_map/ppermute | solution.py:154
  153.8 9.2 %collective-permute-start.35 = (f16[2,64,256]{2,1,0:T(8,128)(2,1)S(1)}, f16[2,64,256]{2,1,0:T(8,128)(2,1)S(1)}, u32[]{:S(2)}, u32[]{:S(2)}) collective-permute-start(f16[2,64,256]{2,1,0:T(8,128)(2,1)S(1)} %reshape.147), channel_id=1, source_target_pairs={{0,6},{1,7},{2,4},{3,5},{4,2},{5,3},{6,0},{7,1},{8,14},{9,15},{10,... | collective-permute-start | bytes 196616 | tf_op jit(solution)/shard_map/ppermute | solution.py:154
  159.7 9.7 %collective-permute-start.40 = (f16[4,2,64,256]{3,2,1,0:T(8,128)(2,1)S(1)}, f16[4,2,64,256]{3,2,1,0:T(8,128)(2,1)S(1)}, u32[]{:S(2)}, u32[]{:S(2)}) collective-permute-start(f16[4,2,64,256]{3,2,1,0:T(8,128)(2,1)S(1)} %get-tuple-element.62), channel_id=1, source_target_pairs={{0,1},{1,0},{2,3},{3,2},{4,5},{5,4},{6,7},{7,6},{8,9},{9,8},{10,11... | collective-permute-start | bytes 786440 | tf_op jit(solution)/shard_map/ppermute | solution.py:154
  163.1 11.2 %collective-permute-start.39 = (f16[4,2,64,256]{3,2,1,0:T(8,128)(2,1)S(1)}, f16[4,2,64,256]{3,2,1,0:T(8,128)(2,1)S(1)}, u32[]{:S(2)}, u32[]{:S(2)}) collective-permute-start(f16[4,2,64,256]{3,2,1,0:T(8,128)(2,1)S(1)} %pad_maximum_fusion.4), channel_id=1, source_target_pairs={{0,1},{1,0},{2,3},{3,2},{4,5},{5,4},{6,7},{7,6},{8,9},{9,8},{10,11... | collective-permute-start | bytes 786440 | tf_op jit(solution)/shard_map/ppermute | solution.py:154
  (24 other events, 182.7 us)
Sparse Core Ops, SparseCore 0:
  10.4 64.2 all-gather.2
where the time goes:
time: 186 us; the launch traced here: 183 us
  waiting for transfers between devices  60.3 us (32%)
  starting transfers between devices  57.6 us (31%)
  Pallas kernels  40.4 us (22%)
  between operations  14.2 us (8%)
  other arithmetic  5.79 us (3%)
  local copies, waits for them, and re-layouts  4.86 us (3%)
    ppermute x41, starting transfers between devices, swap(): return lax.ppermute(array, AXES, [(i, i ^ mask) for i in range(total)])  57.6 us
    ppermute x41, waiting for transfers between devices, swap(): return lax.ppermute(array, AXES, [(i, i ^ mask) for i in range(total)])  55 us
    pallas_call x2, Pallas kernels, ladder_terms(): pl.pallas_call(functools.partial(ladder_kernel, dims), out_shape=(part, p...  36.9 us
    all_gather x1, waiting for transfers between devices, body(): amps.append([lax.all_gather(parts[-1], AXES, axis=0, tiled=False)])  5.31 us
    convert_element_type x2, other arithmetic, add_other_core(): ((keep + got) * scale).astype(jnp.float16)  4.34 us
  transfers between devices with their start and end apart: 42, of which 18 were waited for; matrix products, arithmetic and copies ran while one was open for 4% of the time, Pallas kernels for 20%

commit v1 on v0

--- a/solution.py
+++ b/solution.py
@@ -315,7 +315,9 @@
 
 
 def body(nodes, cores, fitted, fit_mask, tasks, owner_map, partner, amplitudes, pair_energy, virt_energy):
-    scale = 2.0 ** -9
+    tile, aux = amplitudes.shape[3], fitted.shape[1] * nodes * cores
+    largest = 2 * aux * min(tasks.shape[0], owner_map.shape[0]) * tile**2 * 0.09375**2 * 6.0
+    scale = 2.0 ** -math.ceil(math.log2(largest / 65000.0))
     total = nodes * cores
     parts = lower(partner, amplitudes)
     groups = len(parts)
@@ -351,7 +353,7 @@
             if not 0 <= stage < len(stages):
                 continue
             value = results[g][stage]
-            if stage and g + 1 < groups and len(results[g + 1]) > 1:
+            if 0 < stage < 4 and g + 1 < groups and len(results[g + 1]) > 1:
                 value = barrier((value, results[g + 1][-1]))[0]
             results[g].append(stages[stage](value))
     straight = [values[4] for values in results]

time: 186 us -> 181 us (0.973)
  the two profiles are of different devices: /device:TPU:16 before, /device:TPU:0 now
where the time goes in v1:
time: 181 us; the launch traced here: 178 us
  Pallas kernels  58.2 us (32%)
  waiting for transfers between devices  49.8 us (28%)
  starting transfers between devices  45.2 us (25%)
  between operations  14.2 us (8%)
  other arithmetic  5.8 us (3%)
  local copies, waits for them, and re-layouts  5.06 us (3%)
    pallas_call x2, Pallas kernels, ladder_terms(): pl.pallas_call(functools.partial(ladder_kernel, dims), out_shape=(part, p...  54.8 us
    ppermute x41, waiting for transfers between devices, swap(): return lax.ppermute(array, AXES, [(i, i ^ mask) for i in range(total)])  49.8 us
    ppermute x41, starting transfers between devices, swap(): return lax.ppermute(array, AXES, [(i, i ^ mask) for i in range(total)])  45.2 us
    convert_element_type x2, other arithmetic, add_other_core(): ((keep + got) * scale).astype(jnp.float16)  4.34 us
  transfers between devices with their start and end apart: 42, of which 16 were waited for; matrix products, arithmetic and copies ran while one was open for 4% of the time, Pallas kernels for 31%

profile of v1, /device:TPU:0, one launch (start us, length us, event | category | flops | bytes accessed | tf_op | source)
XLA Modules:
  0.0 178.4 jit_solution(6356850078711726197)
XLA Ops:
  6.5 1.8 lower.1
  8.3 3.1 %collective-permute-start = (bf16[2,2,64,256]{3,2,1,0:T(8,128)(2,1)}, bf16[2,2,64,256]{3,2,1,0:T(8,128)(2,1)S(1)}, u32[]{:S(2)}, u32[]{:S(2)}) collective-permute-start(bf16[2,2,64,256]{3,2,1,0:T(8,128)(2,1)} %get-tuple-element.25), channel_id=1, source_target_pairs={{0,2},{1,3},{2,0},{3,1},{4,6},{5,7},{6,4},{7,5},{8,10},{9,11},{10,... | collective-permute-start | bytes 393224 | tf_op jit(solution)/shard_map/ppermute | solution.py:154
  11.4 2.6 %collective-permute-start.1 = (bf16[2,2,64,256]{3,2,1,0:T(8,128)(2,1)}, bf16[2,2,64,256]{3,2,1,0:T(8,128)(2,1)S(1)}, u32[]{:S(2)}, u32[]{:S(2)}) collective-permute-start(bf16[2,2,64,256]{3,2,1,0:T(8,128)(2,1)} %get-tuple-element.25), channel_id=1, source_target_pairs={{0,4},{1,5},{2,6},{3,7},{4,0},{5,1},{6,2},{7,3},{8,12},{9,13},{10,... | collective-permute-start | bytes 393224 | tf_op jit(solution)/shard_map/ppermute | solution.py:154
  14.9 1.7 collective-permute-done
  16.7 7.9 %collective-permute-done.1 = bf16[2,2,64,256]{3,2,1,0:T(8,128)(2,1)S(1)} collective-permute-done((bf16[2,2,64,256]{3,2,1,0:T(8,128)(2,1)}, bf16[2,2,64,256]{3,2,1,0:T(8,128)(2,1)S(1)}, u32[]{:S(2)}, u32[]{:S(2)}) %collective-permute-start.1) | collective-permute-done | bytes 131104 | tf_op jit(solution)/shard_map/ppermute | solution.py:154
  24.7 1.6 collective-permute-start.7
  26.3 1.6 collective-permute-start.3
  27.9 3.2 %collective-permute-done.7 = bf16[4,2,64,256]{3,2,1,0:T(8,128)(2,1)S(1)} collective-permute-done((bf16[4,2,64,256]{3,2,1,0:T(8,128)(2,1)S(1)}, bf16[4,2,64,256]{3,2,1,0:T(8,128)(2,1)S(1)}, u32[]{:S(2)}, u32[]{:S(2)}) %collective-permute-start.7) | collective-permute-done | bytes 262176 | tf_op jit(solution)/shard_map/ppermute | solution.py:154
  32.7 2.0 %collective-permute-done.3 = bf16[4,2,64,256]{3,2,1,0:T(8,128)(2,1)S(1)} collective-permute-done((bf16[4,2,64,256]{3,2,1,0:T(8,128)(2,1)S(1)}, bf16[4,2,64,256]{3,2,1,0:T(8,128)(2,1)S(1)}, u32[]{:S(2)}, u32[]{:S(2)}) %collective-permute-start.3) | collective-permute-done | bytes 262176 | tf_op jit(solution)/shard_map/ppermute | solution.py:154
  35.6 12.1 %collective-permute-done.8.refs_5_ = bf16[2,4,2,64,256]{4,3,2,1,0:T(8,128)(2,1)S(1)} collective-permute-done((bf16[2,4,2,64,256]{4,3,2,1,0:T(8,128)(2,1)S(1)}, bf16[2,4,2,64,256]{4,3,2,1,0:T(8,128)(2,1)S(1)}, u32[]{:S(2)}, u32[]{:S(2)}) %collective-permute-start.8) | collective-permute-done | bytes 524320 | tf_op jit(solution)/shard_map/ppermute | solution.py:154
  50.5 27.4 %ladder.2 = (f32[16,2,64,256]{3,2,1,0:T(8,128)}, f32[16,2,64,256]{3,2,1,0:T(8,128)}) custom-call(s32[16,32]{1,0:T(8,128)} %mask_ref.3, s32[16,2]{1,0:T(8,128)} %copy.43.tasks_ref, s32[16]{0:T(128)} %owner_ref.5, bf16[16,8,256,256]{3,2,1,0:T(8,128)(2,1)} %fitted_ref.3, bf16[2,4,2,64,256]{4,3,2,1,0:T(8,128)(2,1)} %copy-done.7, ...), custom_call_target="tpu_custom_call" | custom-call | flops 20000000000 | bytes 31457280 | tf_op jit(solution)/shard_map/ladder/pallas_call | solution.py:131
  78.1 27.3 %ladder.3 = (f32[16,2,64,256]{3,2,1,0:T(8,128)}, f32[16,2,64,256]{3,2,1,0:T(8,128)}) custom-call(s32[16,32]{1,0:T(8,128)} %mask_ref.3, s32[16,2]{1,0:T(8,128)} %copy.43.tasks_ref, s32[16]{0:T(128)} %owner_ref.5, bf16[16,8,256,256]{3,2,1,0:T(8,128)(2,1)} %fitted_ref.3, bf16[32,2,2,64,256]{4,3,2,1,0:T(8,128)(2,1)} %bitcast.147), custom_call_target="tpu_custom_call" | custom-call | flops 20000000000 | bytes 31457280 | tf_op jit(solution)/shard_map/ladder/pallas_call | solution.py:131
  105.6 2.2 %multiply_convert_fusion.1 = f16[16,2,64,256]{3,2,1,0:T(8,128)(2,1)S(1)} fusion(f32[16,2,64,256]{3,2,1,0:T(8,128)S(1)} %copy-done.4, f32[16,2,64,256]{3,2,1,0:T(8,128)} %collective-permute-done.11), kind=kLoop, calls=%fused_computation.1 | loop fusion | flops 1572864 | bytes 5242880 | tf_op jit(solution)/shard_map/convert_element_type | solution.py:172
  107.8 2.1 %collective-permute-done.12 = f32[16,2,64,256]{3,2,1,0:T(8,128)} collective-permute-done((f32[16,2,64,256]{3,2,1,0:T(8,128)}, f32[16,2,64,256]{3,2,1,0:T(8,128)}, u32[]{:S(2)}, u32[]{:S(2)}) %collective-permute-start.12) | collective-permute-done | bytes 2097184 | tf_op jit(solution)/shard_map/ppermute | solution.py:154
  110.0 2.1 %multiply_convert_fusion = f16[16,2,64,256]{3,2,1,0:T(8,128)(2,1)S(1)} fusion(f32[16,2,64,256]{3,2,1,0:T(8,128)S(1)} %copy-done.5, f32[16,2,64,256]{3,2,1,0:T(8,128)} %collective-permute-done.12), kind=kLoop, calls=%fused_computation | loop fusion | flops 1572864 | bytes 5242880 | tf_op jit(solution)/shard_map/convert_element_type | solution.py:172
  113.1 2.1 %collective-permute-start.15 = (f16[8,2,1,32,256]{4,3,2,1,0:T(8,128)(2,1)S(1)}, f16[8,2,1,32,256]{4,3,2,1,0:T(8,128)(2,1)S(1)}, u32[]{:S(2)}, u32[]{:S(2)}) collective-permute-start(f16[8,2,1,32,256]{4,3,2,1,0:T(8,128)(2,1)S(1)} %constant_dynamic-slice_fusion.14), channel_id=1, source_target_pairs={{0,16},{1,17},{2,18},{3,19},{4,20},{5,21},{6,22},{7,23},{8,24},{9,... | collective-permute-start | bytes 786440 | tf_op jit(solution)/shard_map/ppermute | solution.py:154
  115.6 2.1 %collective-permute-start.13 = (f16[8,2,1,32,256]{4,3,2,1,0:T(8,128)(2,1)S(1)}, f16[8,2,1,32,256]{4,3,2,1,0:T(8,128)(2,1)S(1)}, u32[]{:S(2)}, u32[]{:S(2)}) collective-permute-start(f16[8,2,1,32,256]{4,3,2,1,0:T(8,128)(2,1)S(1)} %constant_dynamic-slice_fusion.17), channel_id=1, source_target_pairs={{0,16},{1,17},{2,18},{3,19},{4,20},{5,21},{6,22},{7,23},{8,24},{9,... | collective-permute-start | bytes 786440 | tf_op jit(solution)/shard_map/ppermute | solution.py:154
  117.6 4.6 %collective-permute-done.16 = f16[4,2,2,32,256]{4,3,1,2,0:T(8,128)(2,1)S(1)} collective-permute-done((f16[4,2,2,32,256]{4,3,1,2,0:T(8,128)(2,1)S(1)}, f16[4,2,2,32,256]{4,3,1,2,0:T(8,128)(2,1)S(1)}, u32[]{:S(2)}, u32[]{:S(2)}) %collective-permute-start.16) | collective-permute-done | bytes 262176 | tf_op jit(solution)/shard_map/ppermute | solution.py:154
  122.5 2.1 %collective-permute-start.20 = (f16[4,2,1,32,256]{4,3,1,2,0:T(8,128)(2,1)S(1)}, f16[4,2,1,32,256]{4,3,1,2,0:T(8,128)(2,1)S(1)}, u32[]{:S(2)}, u32[]{:S(2)}) collective-permute-start(f16[4,2,1,32,256]{4,3,1,2,0:T(8,128)(2,1)S(1)} %constant_dynamic-slice_fusion.10), channel_id=1, source_target_pairs={{0,16},{1,17},{2,18},{3,19},{4,20},{5,21},{6,22},{7,23},{8,24},{9,... | collective-permute-start | bytes 393224 | tf_op jit(solution)/shard_map/ppermute | solution.py:154
  124.7 3.2 %collective-permute-done.13 = f16[8,2,1,32,256]{4,3,2,1,0:T(8,128)(2,1)S(1)} collective-permute-done((f16[8,2,1,32,256]{4,3,2,1,0:T(8,128)(2,1)S(1)}, f16[8,2,1,32,256]{4,3,2,1,0:T(8,128)(2,1)S(1)}, u32[]{:S(2)}, u32[]{:S(2)}) %collective-permute-start.13) | collective-permute-done | bytes 262176 | tf_op jit(solution)/shard_map/ppermute | solution.py:154
  128.2 2.1 %collective-permute-start.18 = (f16[4,2,1,32,256]{4,3,1,2,0:T(8,128)(2,1)S(1)}, f16[4,2,1,32,256]{4,3,1,2,0:T(8,128)(2,1)S(1)}, u32[]{:S(2)}, u32[]{:S(2)}) collective-permute-start(f16[4,2,1,32,256]{4,3,1,2,0:T(8,128)(2,1)S(1)} %constant_dynamic-slice_fusion.11), channel_id=1, source_target_pairs={{0,16},{1,17},{2,18},{3,19},{4,20},{5,21},{6,22},{7,23},{8,24},{9,... | collective-permute-start | bytes 393224 | tf_op jit(solution)/shard_map/ppermute | solution.py:154
  130.9 4.3 %collective-permute-start.26 = (f16[2,64,256]{2,1,0:T(8,128)(2,1)S(1)}, f16[2,64,256]{2,1,0:T(8,128)(2,1)S(1)}, u32[]{:S(2)}, u32[]{:S(2)}) collective-permute-start(f16[2,64,256]{2,1,0:T(8,128)(2,1)S(1)} %get-tuple-element.62), channel_id=1, source_target_pairs={{0,6},{1,7},{2,4},{3,5},{4,2},{5,3},{6,0},{7,1},{8,14},{9,15},{10,... | collective-permute-start | bytes 196616 | tf_op jit(solution)/shard_map/ppermute | solution.py:154
  136.1 4.0 %collective-permute-start.23 = (f16[2,64,256]{2,1,0:T(8,128)(2,1)S(1)}, f16[2,64,256]{2,1,0:T(8,128)(2,1)S(1)}, u32[]{:S(2)}, u32[]{:S(2)}) collective-permute-start(f16[2,64,256]{2,1,0:T(8,128)(2,1)S(1)} %get-tuple-element.65), channel_id=1, source_target_pairs={{0,6},{1,7},{2,4},{3,5},{4,2},{5,3},{6,0},{7,1},{8,14},{9,15},{10,... | collective-permute-start | bytes 196616 | tf_op jit(solution)/shard_map/ppermute | solution.py:154
  140.3 2.0 %collective-permute-start.35 = (f16[64,128]{1,0:T(8,128)(2,1)S(1)}, f16[64,128]{1,0:T(8,128)(2,1)S(1)}, u32[]{:S(2)}, u32[]{:S(2)}) collective-permute-start(f16[64,128]{1,0:T(8,128)(2,1)S(1)} %get-tuple-element.85), channel_id=1, source_target_pairs={{0,16},{1,17},{2,18},{3,19},{4,20},{5,21},{6,22},{7,23},{8,24},{9,... | collective-permute-start | bytes 49160 | tf_op jit(solution)/shard_map/ppermute | solution.py:154
  142.4 1.8 %collective-permute-done.22 = f16[2,64,256]{2,1,0:T(8,128)(2,1)S(1)} collective-permute-done((f16[2,64,256]{2,1,0:T(8,128)(2,1)S(1)}, f16[2,64,256]{2,1,0:T(8,128)(2,1)S(1)}, u32[]{:S(2)}, u32[]{:S(2)}) %collective-permute-start.22) | collective-permute-done | bytes 65568 | tf_op jit(solution)/shard_map/ppermute | solution.py:154
  149.8 1.8 %collective-permute-start.39 = (f16[2,64,256]{2,1,0:T(8,128)(2,1)S(1)}, f16[2,64,256]{2,1,0:T(8,128)(2,1)S(1)}, u32[]{:S(2)}, u32[]{:S(2)}) collective-permute-start(f16[2,64,256]{2,1,0:T(8,128)(2,1)S(1)} %reshape.151), channel_id=1, source_target_pairs={{0,6},{1,7},{2,4},{3,5},{4,2},{5,3},{6,0},{7,1},{8,14},{9,15},{10,... | collective-permute-start | bytes 196616 | tf_op jit(solution)/shard_map/ppermute | solution.py:154
  152.5 2.3 %collective-permute-start.31 = (f16[2,64,256]{2,1,0:T(8,128)(2,1)S(1)}, f16[2,64,256]{2,1,0:T(8,128)(2,1)S(1)}, u32[]{:S(2)}, u32[]{:S(2)}) collective-permute-start(f16[2,64,256]{2,1,0:T(8,128)(2,1)S(1)} %reshape.147), channel_id=1, source_target_pairs={{0,4},{1,5},{2,6},{3,7},{4,0},{5,1},{6,2},{7,3},{8,12},{9,13},{10,... | collective-permute-start | bytes 196616 | tf_op jit(solution)/shard_map/ppermute | solution.py:154
  154.8 1.7 collective-permute-start.32
  156.8 1.7 collective-permute-start.40
  158.6 3.5 %collective-permute-done.31 = f16[2,64,256]{2,1,0:T(8,128)(2,1)S(1)} collective-permute-done((f16[2,64,256]{2,1,0:T(8,128)(2,1)S(1)}, f16[2,64,256]{2,1,0:T(8,128)(2,1)S(1)}, u32[]{:S(2)}, u32[]{:S(2)}) %collective-permute-start.31) | collective-permute-done | bytes 65568 | tf_op jit(solution)/shard_map/ppermute | solution.py:154
  163.9 5.6 %collective-permute-done.33 = f16[4,2,64,256]{3,2,1,0:T(8,128)(2,1)S(1)} collective-permute-done((f16[4,2,64,256]{3,2,1,0:T(8,128)(2,1)S(1)}, f16[4,2,64,256]{3,2,1,0:T(8,128)(2,1)S(1)}, u32[]{:S(2)}, u32[]{:S(2)}) %collective-permute-start.33) | collective-permute-done | bytes 262176 | tf_op jit(solution)/shard_map/ppermute | solution.py:154
  169.8 1.7 update.1
  (149 shorter events, 18.9 us)
Async XLA Ops:
  6.5 71.5 %all-gather.3.cloned.1.call-start = ((), (), s32[]{:S(2)}) async-start(), calls=%async_computation | async-start | bytes 4325376 | tf_op jit(solution)/shard_map/all_gather | solution.py:334
  8.3 8.3 %collective-permute-start = (bf16[2,2,64,256]{3,2,1,0:T(8,128)(2,1)}, bf16[2,2,64,256]{3,2,1,0:T(8,128)(2,1)S(1)}, u32[]{:S(2)}, u32[]{:S(2)}) collective-permute-start(bf16[2,2,64,256]{3,2,1,0:T(8,128)(2,1)} %get-tuple-element.25), channel_id=1, source_target_pairs={{0,2},{1,3},{2,0},{3,1},{4,6},{5,7},{6,4},{7,5},{8,10},{9,11},{10,... | collective-permute-start | bytes 393224 | tf_op jit(solution)/shard_map/ppermute | solution.py:154
  11.4 13.2 %collective-permute-start.1 = (bf16[2,2,64,256]{3,2,1,0:T(8,128)(2,1)}, bf16[2,2,64,256]{3,2,1,0:T(8,128)(2,1)S(1)}, u32[]{:S(2)}, u32[]{:S(2)}) collective-permute-start(bf16[2,2,64,256]{3,2,1,0:T(8,128)(2,1)} %get-tuple-element.25), channel_id=1, source_target_pairs={{0,4},{1,5},{2,6},{3,7},{4,0},{5,1},{6,2},{7,3},{8,12},{9,13},{10,... | collective-permute-start | bytes 393224 | tf_op jit(solution)/shard_map/ppermute | solution.py:154
  14.0 10.6 %collective-permute-start.2 = (bf16[2,2,64,256]{3,2,1,0:T(8,128)(2,1)}, bf16[2,2,64,256]{3,2,1,0:T(8,128)(2,1)S(1)}, u32[]{:S(2)}, u32[]{:S(2)}) collective-permute-start(bf16[2,2,64,256]{3,2,1,0:T(8,128)(2,1)} %get-tuple-element.25), channel_id=1, source_target_pairs={{0,6},{1,7},{2,4},{3,5},{4,2},{5,3},{6,0},{7,1},{8,14},{9,15},{10,... | collective-permute-start | bytes 393224 | tf_op jit(solution)/shard_map/ppermute | solution.py:154
  24.7 6.4 %collective-permute-start.7 = (bf16[4,2,64,256]{3,2,1,0:T(8,128)(2,1)S(1)}, bf16[4,2,64,256]{3,2,1,0:T(8,128)(2,1)S(1)}, u32[]{:S(2)}, u32[]{:S(2)}) collective-permute-start(bf16[4,2,64,256]{3,2,1,0:T(8,128)(2,1)S(1)} %get-tuple-element.68), channel_id=1, source_target_pairs={{0,16},{1,17},{2,18},{3,19},{4,20},{5,21},{6,22},{7,23},{8,24},{9,... | collective-permute-start | bytes 786440 | tf_op jit(solution)/shard_map/ppermute | solution.py:154
  26.3 8.4 %collective-permute-start.3 = (bf16[4,2,64,256]{3,2,1,0:T(8,128)(2,1)S(1)}, bf16[4,2,64,256]{3,2,1,0:T(8,128)(2,1)S(1)}, u32[]{:S(2)}, u32[]{:S(2)}) collective-permute-start(bf16[4,2,64,256]{3,2,1,0:T(8,128)(2,1)S(1)} %get-tuple-element.70), channel_id=1, source_target_pairs={{0,1},{1,0},{2,3},{3,2},{4,5},{5,4},{6,7},{7,6},{8,9},{9,8},{10,11... | collective-permute-start | bytes 786440 | tf_op jit(solution)/shard_map/ppermute | solution.py:154
  31.2 16.5 %collective-permute-start.8 = (bf16[2,4,2,64,256]{4,3,2,1,0:T(8,128)(2,1)S(1)}, bf16[2,4,2,64,256]{4,3,2,1,0:T(8,128)(2,1)S(1)}, u32[]{:S(2)}, u32[]{:S(2)}) collective-permute-start(bf16[2,4,2,64,256]{4,3,2,1,0:T(8,128)(2,1)S(1)} %pad_maximum_fusion.1.refs_4_), channel_id=1, source_target_pairs={{0,1},{1,0},{2,3},{3,2},{4,5},{5,4},{6,7},{7,6},{8,9},{9,8},{10,11... | collective-permute-start | bytes 1572872 | tf_op jit(solution)/shard_map/ppermute | solution.py:154
  34.8 12.9 %collective-permute-start.5 = (bf16[2,4,2,64,256]{4,3,2,1,0:T(8,128)(2,1)S(1)}, bf16[2,4,2,64,256]{4,3,2,1,0:T(8,128)(2,1)S(1)}, u32[]{:S(2)}, u32[]{:S(2)}) collective-permute-start(bf16[2,4,2,64,256]{4,3,2,1,0:T(8,128)(2,1)S(1)} %pad_maximum_fusion.refs_0_), channel_id=1, source_target_pairs={{0,16},{1,17},{2,18},{3,19},{4,20},{5,21},{6,22},{7,23},{8,24},{9,... | collective-permute-start | bytes 1572872 | tf_op jit(solution)/shard_map/ppermute | solution.py:154
  35.1 13.8 %collective-permute-start.4 = (bf16[2,4,2,64,256]{4,3,2,1,0:T(8,128)(2,1)S(1)}, bf16[2,4,2,64,256]{4,3,2,1,0:T(8,128)(2,1)S(1)}, u32[]{:S(2)}, u32[]{:S(2)}) collective-permute-start(bf16[2,4,2,64,256]{4,3,2,1,0:T(8,128)(2,1)S(1)} %pad_maximum_fusion.refs_0_), channel_id=1, source_target_pairs={{0,8},{1,9},{2,10},{3,11},{4,12},{5,13},{6,14},{7,15},{8,0},{9,1},... | collective-permute-start | bytes 1572872 | tf_op jit(solution)/shard_map/ppermute | solution.py:154
  35.1 13.8 %collective-permute-start.9 = (bf16[2,4,2,64,256]{4,3,2,1,0:T(8,128)(2,1)S(1)}, bf16[2,4,2,64,256]{4,3,2,1,0:T(8,128)(2,1)S(1)}, u32[]{:S(2)}, u32[]{:S(2)}) collective-permute-start(bf16[2,4,2,64,256]{4,3,2,1,0:T(8,128)(2,1)S(1)} %pad_maximum_fusion.1.refs_4_), channel_id=1, source_target_pairs={{0,8},{1,9},{2,10},{3,11},{4,12},{5,13},{6,14},{7,15},{8,0},{9,1},... | collective-permute-start | bytes 1572872 | tf_op jit(solution)/shard_map/ppermute | solution.py:154
  78.0 27.6 %collective-permute-start.11 = (f32[16,2,64,256]{3,2,1,0:T(8,128)}, f32[16,2,64,256]{3,2,1,0:T(8,128)}, u32[]{:S(2)}, u32[]{:S(2)}) collective-permute-start(f32[16,2,64,256]{3,2,1,0:T(8,128)} %get-tuple-element.27), channel_id=1, source_target_pairs={{0,8},{1,9},{2,10},{3,11},{4,12},{5,13},{6,14},{7,15},{8,0},{9,1},... | collective-permute-start | bytes 6291464 | tf_op jit(solution)/shard_map/ppermute | solution.py:154
  113.0 9.2 %collective-permute-start.16 = (f16[4,2,2,32,256]{4,3,1,2,0:T(8,128)(2,1)S(1)}, f16[4,2,2,32,256]{4,3,1,2,0:T(8,128)(2,1)S(1)}, u32[]{:S(2)}, u32[]{:S(2)}) collective-permute-start(f16[4,2,2,32,256]{4,3,1,2,0:T(8,128)(2,1)S(1)} %bitcast.125), channel_id=1, source_target_pairs={{0,1},{1,0},{2,3},{3,2},{4,5},{5,4},{6,7},{7,6},{8,9},{9,8},{10,11... | collective-permute-start | bytes 786440 | tf_op jit(solution)/shard_map/ppermute | solution.py:154
  113.1 9.2 %collective-permute-start.15 = (f16[8,2,1,32,256]{4,3,2,1,0:T(8,128)(2,1)S(1)}, f16[8,2,1,32,256]{4,3,2,1,0:T(8,128)(2,1)S(1)}, u32[]{:S(2)}, u32[]{:S(2)}) collective-permute-start(f16[8,2,1,32,256]{4,3,2,1,0:T(8,128)(2,1)S(1)} %constant_dynamic-slice_fusion.14), channel_id=1, source_target_pairs={{0,16},{1,17},{2,18},{3,19},{4,20},{5,21},{6,22},{7,23},{8,24},{9,... | collective-permute-start | bytes 786440 | tf_op jit(solution)/shard_map/ppermute | solution.py:154
  115.4 12.6 %collective-permute-start.14 = (f16[4,2,2,32,256]{4,3,1,2,0:T(8,128)(2,1)S(1)}, f16[4,2,2,32,256]{4,3,1,2,0:T(8,128)(2,1)S(1)}, u32[]{:S(2)}, u32[]{:S(2)}) collective-permute-start(f16[4,2,2,32,256]{4,3,1,2,0:T(8,128)(2,1)S(1)} %bitcast.124), channel_id=1, source_target_pairs={{0,1},{1,0},{2,3},{3,2},{4,5},{5,4},{6,7},{7,6},{8,9},{9,8},{10,11... | collective-permute-start | bytes 786440 | tf_op jit(solution)/shard_map/ppermute | solution.py:154
  115.6 12.4 %collective-permute-start.13 = (f16[8,2,1,32,256]{4,3,2,1,0:T(8,128)(2,1)S(1)}, f16[8,2,1,32,256]{4,3,2,1,0:T(8,128)(2,1)S(1)}, u32[]{:S(2)}, u32[]{:S(2)}) collective-permute-start(f16[8,2,1,32,256]{4,3,2,1,0:T(8,128)(2,1)S(1)} %constant_dynamic-slice_fusion.17), channel_id=1, source_target_pairs={{0,16},{1,17},{2,18},{3,19},{4,20},{5,21},{6,22},{7,23},{8,24},{9,... | collective-permute-start | bytes 786440 | tf_op jit(solution)/shard_map/ppermute | solution.py:154
  122.5 8.0 %collective-permute-start.20 = (f16[4,2,1,32,256]{4,3,1,2,0:T(8,128)(2,1)S(1)}, f16[4,2,1,32,256]{4,3,1,2,0:T(8,128)(2,1)S(1)}, u32[]{:S(2)}, u32[]{:S(2)}) collective-permute-start(f16[4,2,1,32,256]{4,3,1,2,0:T(8,128)(2,1)S(1)} %constant_dynamic-slice_fusion.10), channel_id=1, source_target_pairs={{0,16},{1,17},{2,18},{3,19},{4,20},{5,21},{6,22},{7,23},{8,24},{9,... | collective-permute-start | bytes 393224 | tf_op jit(solution)/shard_map/ppermute | solution.py:154
  128.2 7.0 %collective-permute-start.18 = (f16[4,2,1,32,256]{4,3,1,2,0:T(8,128)(2,1)S(1)}, f16[4,2,1,32,256]{4,3,1,2,0:T(8,128)(2,1)S(1)}, u32[]{:S(2)}, u32[]{:S(2)}) collective-permute-start(f16[4,2,1,32,256]{4,3,1,2,0:T(8,128)(2,1)S(1)} %constant_dynamic-slice_fusion.11), channel_id=1, source_target_pairs={{0,16},{1,17},{2,18},{3,19},{4,20},{5,21},{6,22},{7,23},{8,24},{9,... | collective-permute-start | bytes 393224 | tf_op jit(solution)/shard_map/ppermute | solution.py:154
  130.8 9.2 %collective-permute-start.25 = (f16[2,64,256]{2,1,0:T(8,128)(2,1)S(1)}, f16[2,64,256]{2,1,0:T(8,128)(2,1)S(1)}, u32[]{:S(2)}, u32[]{:S(2)}) collective-permute-start(f16[2,64,256]{2,1,0:T(8,128)(2,1)S(1)} %get-tuple-element.63), channel_id=1, source_target_pairs={{0,4},{1,5},{2,6},{3,7},{4,0},{5,1},{6,2},{7,3},{8,12},{9,13},{10,... | collective-permute-start | bytes 196616 | tf_op jit(solution)/shard_map/ppermute | solution.py:154
  130.9 9.1 %collective-permute-start.26 = (f16[2,64,256]{2,1,0:T(8,128)(2,1)S(1)}, f16[2,64,256]{2,1,0:T(8,128)(2,1)S(1)}, u32[]{:S(2)}, u32[]{:S(2)}) collective-permute-start(f16[2,64,256]{2,1,0:T(8,128)(2,1)S(1)} %get-tuple-element.62), channel_id=1, source_target_pairs={{0,6},{1,7},{2,4},{3,5},{4,2},{5,3},{6,0},{7,1},{8,14},{9,15},{10,... | collective-permute-start | bytes 196616 | tf_op jit(solution)/shard_map/ppermute | solution.py:154
  135.6 6.7 %collective-permute-start.21 = (f16[2,64,256]{2,1,0:T(8,128)(2,1)S(1)}, f16[2,64,256]{2,1,0:T(8,128)(2,1)S(1)}, u32[]{:S(2)}, u32[]{:S(2)}) collective-permute-start(f16[2,64,256]{2,1,0:T(8,128)(2,1)S(1)} %get-tuple-element.64), channel_id=1, source_target_pairs={{0,2},{1,3},{2,0},{3,1},{4,6},{5,7},{6,4},{7,5},{8,10},{9,11},{10,... | collective-permute-start | bytes 196616 | tf_op jit(solution)/shard_map/ppermute | solution.py:154
  135.6 8.5 %collective-permute-start.22 = (f16[2,64,256]{2,1,0:T(8,128)(2,1)S(1)}, f16[2,64,256]{2,1,0:T(8,128)(2,1)S(1)}, u32[]{:S(2)}, u32[]{:S(2)}) collective-permute-start(f16[2,64,256]{2,1,0:T(8,128)(2,1)S(1)} %get-tuple-element.66), channel_id=1, source_target_pairs={{0,4},{1,5},{2,6},{3,7},{4,0},{5,1},{6,2},{7,3},{8,12},{9,13},{10,... | collective-permute-start | bytes 196616 | tf_op jit(solution)/shard_map/ppermute | solution.py:154
  136.1 8.1 %collective-permute-start.23 = (f16[2,64,256]{2,1,0:T(8,128)(2,1)S(1)}, f16[2,64,256]{2,1,0:T(8,128)(2,1)S(1)}, u32[]{:S(2)}, u32[]{:S(2)}) collective-permute-start(f16[2,64,256]{2,1,0:T(8,128)(2,1)S(1)} %get-tuple-element.65), channel_id=1, source_target_pairs={{0,6},{1,7},{2,4},{3,5},{4,2},{5,3},{6,0},{7,1},{8,14},{9,15},{10,... | collective-permute-start | bytes 196616 | tf_op jit(solution)/shard_map/ppermute | solution.py:154
  140.3 6.0 %collective-permute-start.35 = (f16[64,128]{1,0:T(8,128)(2,1)S(1)}, f16[64,128]{1,0:T(8,128)(2,1)S(1)}, u32[]{:S(2)}, u32[]{:S(2)}) collective-permute-start(f16[64,128]{1,0:T(8,128)(2,1)S(1)} %get-tuple-element.85), channel_id=1, source_target_pairs={{0,16},{1,17},{2,18},{3,19},{4,20},{5,21},{6,22},{7,23},{8,24},{9,... | collective-permute-start | bytes 49160 | tf_op jit(solution)/shard_map/ppermute | solution.py:154
  144.5 7.1 %collective-permute-start.28 = (f16[64,128]{1,0:T(8,128)(2,1)S(1)}, f16[64,128]{1,0:T(8,128)(2,1)S(1)}, u32[]{:S(2)}, u32[]{:S(2)}) collective-permute-start(f16[64,128]{1,0:T(8,128)(2,1)S(1)} %get-tuple-element.93), channel_id=1, source_target_pairs={{0,16},{1,17},{2,18},{3,19},{4,20},{5,21},{6,22},{7,23},{8,24},{9,... | collective-permute-start | bytes 49160 | tf_op jit(solution)/shard_map/ppermute | solution.py:154
  146.9 8.0 %collective-permute-start.37 = (f16[2,64,256]{2,1,0:T(8,128)(2,1)S(1)}, f16[2,64,256]{2,1,0:T(8,128)(2,1)S(1)}, u32[]{:S(2)}, u32[]{:S(2)}) collective-permute-start(f16[2,64,256]{2,1,0:T(8,128)(2,1)S(1)} %reshape.151), channel_id=1, source_target_pairs={{0,2},{1,3},{2,0},{3,1},{4,6},{5,7},{6,4},{7,5},{8,10},{9,11},{10,... | collective-permute-start | bytes 196616 | tf_op jit(solution)/shard_map/ppermute | solution.py:154
  148.2 8.5 %collective-permute-start.38 = (f16[2,64,256]{2,1,0:T(8,128)(2,1)S(1)}, f16[2,64,256]{2,1,0:T(8,128)(2,1)S(1)}, u32[]{:S(2)}, u32[]{:S(2)}) collective-permute-start(f16[2,64,256]{2,1,0:T(8,128)(2,1)S(1)} %reshape.151), channel_id=1, source_target_pairs={{0,4},{1,5},{2,6},{3,7},{4,0},{5,1},{6,2},{7,3},{8,12},{9,13},{10,... | collective-permute-start | bytes 196616 | tf_op jit(solution)/shard_map/ppermute | solution.py:154
  149.8 6.9 %collective-permute-start.39 = (f16[2,64,256]{2,1,0:T(8,128)(2,1)S(1)}, f16[2,64,256]{2,1,0:T(8,128)(2,1)S(1)}, u32[]{:S(2)}, u32[]{:S(2)}) collective-permute-start(f16[2,64,256]{2,1,0:T(8,128)(2,1)S(1)} %reshape.151), channel_id=1, source_target_pairs={{0,6},{1,7},{2,4},{3,5},{4,2},{5,3},{6,0},{7,1},{8,14},{9,15},{10,... | collective-permute-start | bytes 196616 | tf_op jit(solution)/shard_map/ppermute | solution.py:154
  152.1 6.5 %collective-permute-start.30 = (f16[2,64,256]{2,1,0:T(8,128)(2,1)S(1)}, f16[2,64,256]{2,1,0:T(8,128)(2,1)S(1)}, u32[]{:S(2)}, u32[]{:S(2)}) collective-permute-start(f16[2,64,256]{2,1,0:T(8,128)(2,1)S(1)} %reshape.147), channel_id=1, source_target_pairs={{0,2},{1,3},{2,0},{3,1},{4,6},{5,7},{6,4},{7,5},{8,10},{9,11},{10,... | collective-permute-start | bytes 196616 | tf_op jit(solution)/shard_map/ppermute | solution.py:154
  152.5 9.6 %collective-permute-start.31 = (f16[2,64,256]{2,1,0:T(8,128)(2,1)S(1)}, f16[2,64,256]{2,1,0:T(8,128)(2,1)S(1)}, u32[]{:S(2)}, u32[]{:S(2)}) collective-permute-start(f16[2,64,256]{2,1,0:T(8,128)(2,1)S(1)} %reshape.147), channel_id=1, source_target_pairs={{0,4},{1,5},{2,6},{3,7},{4,0},{5,1},{6,2},{7,3},{8,12},{9,13},{10,... | collective-permute-start | bytes 196616 | tf_op jit(solution)/shard_map/ppermute | solution.py:154
  154.8 7.3 %collective-permute-start.32 = (f16[2,64,256]{2,1,0:T(8,128)(2,1)S(1)}, f16[2,64,256]{2,1,0:T(8,128)(2,1)S(1)}, u32[]{:S(2)}, u32[]{:S(2)}) collective-permute-start(f16[2,64,256]{2,1,0:T(8,128)(2,1)S(1)} %reshape.147), channel_id=1, source_target_pairs={{0,6},{1,7},{2,4},{3,5},{4,2},{5,3},{6,0},{7,1},{8,14},{9,15},{10,... | collective-permute-start | bytes 196616 | tf_op jit(solution)/shard_map/ppermute | solution.py:154
  156.8 6.8 %collective-permute-start.40 = (f16[4,2,64,256]{3,2,1,0:T(8,128)(2,1)S(1)}, f16[4,2,64,256]{3,2,1,0:T(8,128)(2,1)S(1)}, u32[]{:S(2)}, u32[]{:S(2)}) collective-permute-start(f16[4,2,64,256]{3,2,1,0:T(8,128)(2,1)S(1)} %get-tuple-element.58), channel_id=1, source_target_pairs={{0,1},{1,0},{2,3},{3,2},{4,5},{5,4},{6,7},{7,6},{8,9},{9,8},{10,11... | collective-permute-start | bytes 786440 | tf_op jit(solution)/shard_map/ppermute | solution.py:154
  162.2 7.3 %collective-permute-start.33 = (f16[4,2,64,256]{3,2,1,0:T(8,128)(2,1)S(1)}, f16[4,2,64,256]{3,2,1,0:T(8,128)(2,1)S(1)}, u32[]{:S(2)}, u32[]{:S(2)}) collective-permute-start(f16[4,2,64,256]{3,2,1,0:T(8,128)(2,1)S(1)} %get-tuple-element.60), channel_id=1, source_target_pairs={{0,1},{1,0},{2,3},{3,2},{4,5},{5,4},{6,7},{7,6},{8,9},{9,8},{10,11... | collective-permute-start | bytes 786440 | tf_op jit(solution)/shard_map/ppermute | solution.py:154
  (24 other events, 196.3 us)
Sparse Core Ops, SparseCore 0:
  10.4 66.1 all-gather.2

commit v2 on v1

--- a/solution.py
+++ b/solution.py
@@ -42,6 +42,11 @@
 
     def start_loads(i, slot):
         _, _, left, right, in_tile = indices(work[i])
+        pltpu.make_async_copy(fitted_ref.at[left], left_buf.at[slot], load_sems.at[slot, 0]).start()
+        for q in range(aux):
+            pltpu.make_async_copy(
+                fitted_ref.at[right, q], right_buf.at[slot, :, pl.ds(q * tile, tile)], load_sems.at[slot, 1]
+            ).start()
         place = slot_of[in_tile]
         inside = place % slots_here
         owner = place // slots_here
@@ -67,11 +72,6 @@
                         source = second_refs[(other % 2) * 2 + x].at[other // 2, far, inside]
                         fetch(source, 1, node_index ^ other)
 
-        pltpu.make_async_copy(fitted_ref.at[left], left_buf.at[slot], load_sems.at[slot, 0]).start()
-        for q in range(aux):
-            pltpu.make_async_copy(
-                fitted_ref.at[right, q], right_buf.at[slot, :, pl.ds(q * tile, tile)], load_sems.at[slot, 1]
-            ).start()
 
     def wait_loads(slot):
         for k, buf in enumerate((left_buf, right_buf, tile_buf)):

time: 181 us -> 179 us (0.989)
  Pallas kernels: 58.2 us -> 27.8 us
  starting transfers between devices: 45.2 us -> 60.9 us
  waiting for transfers between devices: 49.8 us -> 63.7 us
    pallas_call x2, Pallas kernels: 54.8 us -> 24.3 us  [ladder_terms(): pl.pallas_call(functools.partial(ladder_kernel, dims), out_shape=(part, p...]
    ppermute x41, starting transfers between devices: 45.2 us -> 60.9 us  [swap(): return lax.ppermute(array, AXES, [(i, i ^ mask) for i in range(total)])]
    all_gather x1, waiting for transfers between devices: 0.02 us -> 13.9 us  [body(): amps.append([lax.all_gather(parts[-1], AXES, axis=0, tiled=False)])]
  transfers between devices with their start and end apart: 42 -> 42, of which waited for: 16 -> 19; matrix products, arithmetic and copies ran while one was open for 4% -> 4% of each run, Pallas kernels for 31% -> 14%
where the time goes in v2:
time: 179 us; the launch traced here: 177 us
  waiting for transfers between devices  63.7 us (36%)
  starting transfers between devices  60.9 us (34%)
  Pallas kernels  27.8 us (16%)
  between operations  14.2 us (8%)
  other arithmetic  5.8 us (3%)
  local copies, waits for them, and re-layouts  5.05 us (3%)
    ppermute x41, starting transfers between devices, swap(): return lax.ppermute(array, AXES, [(i, i ^ mask) for i in range(total)])  60.9 us
    ppermute x41, waiting for transfers between devices, swap(): return lax.ppermute(array, AXES, [(i, i ^ mask) for i in range(total)])  49.7 us
    pallas_call x2, Pallas kernels, ladder_terms(): pl.pallas_call(functools.partial(ladder_kernel, dims), out_shape=(part, p...  24.3 us
    all_gather x1, waiting for transfers between devices, body(): amps.append([lax.all_gather(parts[-1], AXES, axis=0, tiled=False)])  13.9 us
    convert_element_type x2, other arithmetic, add_other_core(): ((keep + got) * scale).astype(jnp.float16)  4.34 us
  transfers between devices with their start and end apart: 42, of which 19 were waited for; matrix products, arithmetic and copies ran while one was open for 4% of the time, Pallas kernels for 14%

profile of v2, /device:TPU:0, one launch (start us, length us, event | category | flops | bytes accessed | tf_op | source)
XLA Modules:
  0.0 177.4 jit_solution(16539357630467787855)
XLA Ops:
  6.5 1.8 %lower.1 = (bf16[2,2,64,256]{3,2,1,0:T(8,128)(2,1)}, bf16[2,2,64,256]{3,2,1,0:T(8,128)(2,1)}) custom-call(s32[4]{0:T(128)} %partner_ref.3, f32[2,4,64,256]{3,2,1,0:T(8,128)} %amps_ref.3), custom_call_target="tpu_custom_call" | custom-call | tf_op jit(solution)/shard_map/lower/pallas_call | solution.py:216
  8.3 3.1 %collective-permute-start = (bf16[2,2,64,256]{3,2,1,0:T(8,128)(2,1)}, bf16[2,2,64,256]{3,2,1,0:T(8,128)(2,1)S(1)}, u32[]{:S(2)}, u32[]{:S(2)}) collective-permute-start(bf16[2,2,64,256]{3,2,1,0:T(8,128)(2,1)} %get-tuple-element.25), channel_id=1, source_target_pairs={{0,2},{1,3},{2,0},{3,1},{4,6},{5,7},{6,4},{7,5},{8,10},{9,11},{10,... | collective-permute-start | bytes 393224 | tf_op jit(solution)/shard_map/ppermute | solution.py:154
  11.4 2.6 %collective-permute-start.1 = (bf16[2,2,64,256]{3,2,1,0:T(8,128)(2,1)}, bf16[2,2,64,256]{3,2,1,0:T(8,128)(2,1)S(1)}, u32[]{:S(2)}, u32[]{:S(2)}) collective-permute-start(bf16[2,2,64,256]{3,2,1,0:T(8,128)(2,1)} %get-tuple-element.25), channel_id=1, source_target_pairs={{0,4},{1,5},{2,6},{3,7},{4,0},{5,1},{6,2},{7,3},{8,12},{9,13},{10,... | collective-permute-start | bytes 393224 | tf_op jit(solution)/shard_map/ppermute | solution.py:154
  14.9 1.7 collective-permute-done
  16.7 7.9 %collective-permute-done.1 = bf16[2,2,64,256]{3,2,1,0:T(8,128)(2,1)S(1)} collective-permute-done((bf16[2,2,64,256]{3,2,1,0:T(8,128)(2,1)}, bf16[2,2,64,256]{3,2,1,0:T(8,128)(2,1)S(1)}, u32[]{:S(2)}, u32[]{:S(2)}) %collective-permute-start.1) | collective-permute-done | bytes 131104 | tf_op jit(solution)/shard_map/ppermute | solution.py:154
  24.7 1.6 collective-permute-start.7
  26.3 1.6 collective-permute-start.3
  27.9 3.2 %collective-permute-done.7 = bf16[4,2,64,256]{3,2,1,0:T(8,128)(2,1)S(1)} collective-permute-done((bf16[4,2,64,256]{3,2,1,0:T(8,128)(2,1)S(1)}, bf16[4,2,64,256]{3,2,1,0:T(8,128)(2,1)S(1)}, u32[]{:S(2)}, u32[]{:S(2)}) %collective-permute-start.7) | collective-permute-done | bytes 262176 | tf_op jit(solution)/shard_map/ppermute | solution.py:154
  32.7 2.0 %collective-permute-done.3 = bf16[4,2,64,256]{3,2,1,0:T(8,128)(2,1)S(1)} collective-permute-done((bf16[4,2,64,256]{3,2,1,0:T(8,128)(2,1)S(1)}, bf16[4,2,64,256]{3,2,1,0:T(8,128)(2,1)S(1)}, u32[]{:S(2)}, u32[]{:S(2)}) %collective-permute-start.3) | collective-permute-done | bytes 262176 | tf_op jit(solution)/shard_map/ppermute | solution.py:154
  35.6 12.1 %collective-permute-done.8.refs_5_ = bf16[2,4,2,64,256]{4,3,2,1,0:T(8,128)(2,1)S(1)} collective-permute-done((bf16[2,4,2,64,256]{4,3,2,1,0:T(8,128)(2,1)S(1)}, bf16[2,4,2,64,256]{4,3,2,1,0:T(8,128)(2,1)S(1)}, u32[]{:S(2)}, u32[]{:S(2)}) %collective-permute-start.8) | collective-permute-done | bytes 524320 | tf_op jit(solution)/shard_map/ppermute | solution.py:154
  50.5 12.0 %ladder.2 = (f32[16,2,64,256]{3,2,1,0:T(8,128)}, f32[16,2,64,256]{3,2,1,0:T(8,128)}) custom-call(s32[16,32]{1,0:T(8,128)} %mask_ref.3, s32[16,2]{1,0:T(8,128)} %copy.43.tasks_ref, s32[16]{0:T(128)} %owner_ref.5, bf16[16,8,256,256]{3,2,1,0:T(8,128)(2,1)} %fitted_ref.3, bf16[2,4,2,64,256]{4,3,2,1,0:T(8,128)(2,1)} %copy-done.7, ...), custom_call_target="tpu_custom_call" | custom-call | flops 20000000000 | bytes 31457280 | tf_op jit(solution)/shard_map/ladder/pallas_call | solution.py:131
  62.6 13.9 %all-gather.3.cloned.1.call-done = bf16[64,2,64,256]{3,2,1,0:T(8,128)(2,1)} async-done(((bf16[2,2,64,256]{3,2,1,0:T(8,128)(2,1)}), bf16[64,2,64,256]{3,2,1,0:T(8,128)(2,1)}) %all-gather.3.cloned.1.call-update) | async-done | bytes 4194320 | tf_op jit(solution)/shard_map/all_gather | solution.py:334
  76.5 12.3 %ladder.3 = (f32[16,2,64,256]{3,2,1,0:T(8,128)}, f32[16,2,64,256]{3,2,1,0:T(8,128)}) custom-call(s32[16,32]{1,0:T(8,128)} %mask_ref.3, s32[16,2]{1,0:T(8,128)} %copy.43.tasks_ref, s32[16]{0:T(128)} %owner_ref.5, bf16[16,8,256,256]{3,2,1,0:T(8,128)(2,1)} %fitted_ref.3, bf16[32,2,2,64,256]{4,3,2,1,0:T(8,128)(2,1)} %bitcast.147), custom_call_target="tpu_custom_call" | custom-call | flops 20000000000 | bytes 31457280 | tf_op jit(solution)/shard_map/ladder/pallas_call | solution.py:131
  89.1 2.2 %multiply_convert_fusion.1 = f16[16,2,64,256]{3,2,1,0:T(8,128)(2,1)S(1)} fusion(f32[16,2,64,256]{3,2,1,0:T(8,128)S(1)} %copy-done.4, f32[16,2,64,256]{3,2,1,0:T(8,128)} %collective-permute-done.11), kind=kLoop, calls=%fused_computation.1 | loop fusion | flops 1572864 | bytes 5242880 | tf_op jit(solution)/shard_map/convert_element_type | solution.py:172
  91.3 2.1 %collective-permute-done.12 = f32[16,2,64,256]{3,2,1,0:T(8,128)} collective-permute-done((f32[16,2,64,256]{3,2,1,0:T(8,128)}, f32[16,2,64,256]{3,2,1,0:T(8,128)}, u32[]{:S(2)}, u32[]{:S(2)}) %collective-permute-start.12) | collective-permute-done | bytes 2097184 | tf_op jit(solution)/shard_map/ppermute | solution.py:154
  93.5 2.1 %multiply_convert_fusion = f16[16,2,64,256]{3,2,1,0:T(8,128)(2,1)S(1)} fusion(f32[16,2,64,256]{3,2,1,0:T(8,128)S(1)} %copy-done.5, f32[16,2,64,256]{3,2,1,0:T(8,128)} %collective-permute-done.12), kind=kLoop, calls=%fused_computation | loop fusion | flops 1572864 | bytes 5242880 | tf_op jit(solution)/shard_map/convert_element_type | solution.py:172
  96.5 13.0 %collective-permute-start.16 = (f16[4,2,2,32,256]{4,3,1,2,0:T(8,128)(2,1)S(1)}, f16[4,2,2,32,256]{4,3,1,2,0:T(8,128)(2,1)S(1)}, u32[]{:S(2)}, u32[]{:S(2)}) collective-permute-start(f16[4,2,2,32,256]{4,3,1,2,0:T(8,128)(2,1)S(1)} %bitcast.125), channel_id=1, source_target_pairs={{0,1},{1,0},{2,3},{3,2},{4,5},{5,4},{6,7},{7,6},{8,9},{9,8},{10,11... | collective-permute-start | bytes 786440 | tf_op jit(solution)/shard_map/ppermute | solution.py:154
  109.6 3.8 %collective-permute-start.15 = (f16[8,2,1,32,256]{4,3,2,1,0:T(8,128)(2,1)S(1)}, f16[8,2,1,32,256]{4,3,2,1,0:T(8,128)(2,1)S(1)}, u32[]{:S(2)}, u32[]{:S(2)}) collective-permute-start(f16[8,2,1,32,256]{4,3,2,1,0:T(8,128)(2,1)S(1)} %constant_dynamic-slice_fusion.14), channel_id=1, source_target_pairs={{0,16},{1,17},{2,18},{3,19},{4,20},{5,21},{6,22},{7,23},{8,24},{9,... | collective-permute-start | bytes 786440 | tf_op jit(solution)/shard_map/ppermute | solution.py:154
  113.6 2.1 %collective-permute-start.14 = (f16[4,2,2,32,256]{4,3,1,2,0:T(8,128)(2,1)S(1)}, f16[4,2,2,32,256]{4,3,1,2,0:T(8,128)(2,1)S(1)}, u32[]{:S(2)}, u32[]{:S(2)}) collective-permute-start(f16[4,2,2,32,256]{4,3,1,2,0:T(8,128)(2,1)S(1)} %bitcast.124), channel_id=1, source_target_pairs={{0,1},{1,0},{2,3},{3,2},{4,5},{5,4},{6,7},{7,6},{8,9},{9,8},{10,11... | collective-permute-start | bytes 786440 | tf_op jit(solution)/shard_map/ppermute | solution.py:154
  116.5 4.0 %collective-permute-done.15 = f16[8,2,1,32,256]{4,3,2,1,0:T(8,128)(2,1)S(1)} collective-permute-done((f16[8,2,1,32,256]{4,3,2,1,0:T(8,128)(2,1)S(1)}, f16[8,2,1,32,256]{4,3,2,1,0:T(8,128)(2,1)S(1)}, u32[]{:S(2)}, u32[]{:S(2)}) %collective-permute-start.15) | collective-permute-done | bytes 262176 | tf_op jit(solution)/shard_map/ppermute | solution.py:154
  120.6 2.1 %collective-permute-start.20 = (f16[4,2,1,32,256]{4,3,1,2,0:T(8,128)(2,1)S(1)}, f16[4,2,1,32,256]{4,3,1,2,0:T(8,128)(2,1)S(1)}, u32[]{:S(2)}, u32[]{:S(2)}) collective-permute-start(f16[4,2,1,32,256]{4,3,1,2,0:T(8,128)(2,1)S(1)} %constant_dynamic-slice_fusion.10), channel_id=1, source_target_pairs={{0,16},{1,17},{2,18},{3,19},{4,20},{5,21},{6,22},{7,23},{8,24},{9,... | collective-permute-start | bytes 393224 | tf_op jit(solution)/shard_map/ppermute | solution.py:154
  122.8 2.1 %collective-permute-start.19 = (f16[4,2,1,32,256]{4,3,1,2,0:T(8,128)(2,1)S(1)}, f16[4,2,1,32,256]{4,3,1,2,0:T(8,128)(2,1)S(1)}, u32[]{:S(2)}, u32[]{:S(2)}) collective-permute-start(f16[4,2,1,32,256]{4,3,1,2,0:T(8,128)(2,1)S(1)} %dynamic-slice_bitcast_fusion), channel_id=1, source_target_pairs={{0,1},{1,0},{2,3},{3,2},{4,5},{5,4},{6,7},{7,6},{8,9},{9,8},{10,11... | collective-permute-start | bytes 393224 | tf_op jit(solution)/shard_map/ppermute | solution.py:154
  126.3 2.1 %collective-permute-start.18 = (f16[4,2,1,32,256]{4,3,1,2,0:T(8,128)(2,1)S(1)}, f16[4,2,1,32,256]{4,3,1,2,0:T(8,128)(2,1)S(1)}, u32[]{:S(2)}, u32[]{:S(2)}) collective-permute-start(f16[4,2,1,32,256]{4,3,1,2,0:T(8,128)(2,1)S(1)} %constant_dynamic-slice_fusion.11), channel_id=1, source_target_pairs={{0,16},{1,17},{2,18},{3,19},{4,20},{5,21},{6,22},{7,23},{8,24},{9,... | collective-permute-start | bytes 393224 | tf_op jit(solution)/shard_map/ppermute | solution.py:154
  128.5 2.1 %collective-permute-start.17 = (f16[4,2,1,32,256]{4,3,1,2,0:T(8,128)(2,1)S(1)}, f16[4,2,1,32,256]{4,3,1,2,0:T(8,128)(2,1)S(1)}, u32[]{:S(2)}, u32[]{:S(2)}) collective-permute-start(f16[4,2,1,32,256]{4,3,1,2,0:T(8,128)(2,1)S(1)} %dynamic-slice_bitcast_fusion.1), channel_id=1, source_target_pairs={{0,1},{1,0},{2,3},{3,2},{4,5},{5,4},{6,7},{7,6},{8,9},{9,8},{10,11... | collective-permute-start | bytes 393224 | tf_op jit(solution)/shard_map/ppermute | solution.py:154
  131.0 4.3 %collective-permute-start.26 = (f16[2,64,256]{2,1,0:T(8,128)(2,1)S(1)}, f16[2,64,256]{2,1,0:T(8,128)(2,1)S(1)}, u32[]{:S(2)}, u32[]{:S(2)}) collective-permute-start(f16[2,64,256]{2,1,0:T(8,128)(2,1)S(1)} %get-tuple-element.62), channel_id=1, source_target_pairs={{0,6},{1,7},{2,4},{3,5},{4,2},{5,3},{6,0},{7,1},{8,14},{9,15},{10,... | collective-permute-start | bytes 196616 | tf_op jit(solution)/shard_map/ppermute | solution.py:154
  136.9 3.1 %collective-permute-start.23 = (f16[2,64,256]{2,1,0:T(8,128)(2,1)S(1)}, f16[2,64,256]{2,1,0:T(8,128)(2,1)S(1)}, u32[]{:S(2)}, u32[]{:S(2)}) collective-permute-start(f16[2,64,256]{2,1,0:T(8,128)(2,1)S(1)} %get-tuple-element.65), channel_id=1, source_target_pairs={{0,6},{1,7},{2,4},{3,5},{4,2},{5,3},{6,0},{7,1},{8,14},{9,15},{10,... | collective-permute-start | bytes 196616 | tf_op jit(solution)/shard_map/ppermute | solution.py:154
  140.6 1.6 collective-permute-start.36
  147.3 2.1 %collective-permute-start.38 = (f16[2,64,256]{2,1,0:T(8,128)(2,1)S(1)}, f16[2,64,256]{2,1,0:T(8,128)(2,1)S(1)}, u32[]{:S(2)}, u32[]{:S(2)}) collective-permute-start(f16[2,64,256]{2,1,0:T(8,128)(2,1)S(1)} %reshape.151), channel_id=1, source_target_pairs={{0,4},{1,5},{2,6},{3,7},{4,0},{5,1},{6,2},{7,3},{8,12},{9,13},{10,... | collective-permute-start | bytes 196616 | tf_op jit(solution)/shard_map/ppermute | solution.py:154
  151.6 3.0 %collective-permute-start.31 = (f16[2,64,256]{2,1,0:T(8,128)(2,1)S(1)}, f16[2,64,256]{2,1,0:T(8,128)(2,1)S(1)}, u32[]{:S(2)}, u32[]{:S(2)}) collective-permute-start(f16[2,64,256]{2,1,0:T(8,128)(2,1)S(1)} %reshape.147), channel_id=1, source_target_pairs={{0,4},{1,5},{2,6},{3,7},{4,0},{5,1},{6,2},{7,3},{8,12},{9,13},{10,... | collective-permute-start | bytes 196616 | tf_op jit(solution)/shard_map/ppermute | solution.py:154
  156.9 4.3 %collective-permute-done.31 = f16[2,64,256]{2,1,0:T(8,128)(2,1)S(1)} collective-permute-done((f16[2,64,256]{2,1,0:T(8,128)(2,1)S(1)}, f16[2,64,256]{2,1,0:T(8,128)(2,1)S(1)}, u32[]{:S(2)}, u32[]{:S(2)}) %collective-permute-start.31) | collective-permute-done | bytes 65568 | tf_op jit(solution)/shard_map/ppermute | solution.py:154
  164.0 4.7 %collective-permute-done.33 = f16[4,2,64,256]{3,2,1,0:T(8,128)(2,1)S(1)} collective-permute-done((f16[4,2,64,256]{3,2,1,0:T(8,128)(2,1)S(1)}, f16[4,2,64,256]{3,2,1,0:T(8,128)(2,1)S(1)}, u32[]{:S(2)}, u32[]{:S(2)}) %collective-permute-start.33) | collective-permute-done | bytes 262176 | tf_op jit(solution)/shard_map/ppermute | solution.py:154
  168.9 1.7 update.1
  (149 shorter events, 24.8 us)
Async XLA Ops:
  6.5 70.0 %all-gather.3.cloned.1.call-start = ((), (), s32[]{:S(2)}) async-start(), calls=%async_computation | async-start | bytes 4325376 | tf_op jit(solution)/shard_map/all_gather | solution.py:334
  8.3 8.3 %collective-permute-start = (bf16[2,2,64,256]{3,2,1,0:T(8,128)(2,1)}, bf16[2,2,64,256]{3,2,1,0:T(8,128)(2,1)S(1)}, u32[]{:S(2)}, u32[]{:S(2)}) collective-permute-start(bf16[2,2,64,256]{3,2,1,0:T(8,128)(2,1)} %get-tuple-element.25), channel_id=1, source_target_pairs={{0,2},{1,3},{2,0},{3,1},{4,6},{5,7},{6,4},{7,5},{8,10},{9,11},{10,... | collective-permute-start | bytes 393224 | tf_op jit(solution)/shard_map/ppermute | solution.py:154
  11.4 13.2 %collective-permute-start.1 = (bf16[2,2,64,256]{3,2,1,0:T(8,128)(2,1)}, bf16[2,2,64,256]{3,2,1,0:T(8,128)(2,1)S(1)}, u32[]{:S(2)}, u32[]{:S(2)}) collective-permute-start(bf16[2,2,64,256]{3,2,1,0:T(8,128)(2,1)} %get-tuple-element.25), channel_id=1, source_target_pairs={{0,4},{1,5},{2,6},{3,7},{4,0},{5,1},{6,2},{7,3},{8,12},{9,13},{10,... | collective-permute-start | bytes 393224 | tf_op jit(solution)/shard_map/ppermute | solution.py:154
  14.0 10.6 %collective-permute-start.2 = (bf16[2,2,64,256]{3,2,1,0:T(8,128)(2,1)}, bf16[2,2,64,256]{3,2,1,0:T(8,128)(2,1)S(1)}, u32[]{:S(2)}, u32[]{:S(2)}) collective-permute-start(bf16[2,2,64,256]{3,2,1,0:T(8,128)(2,1)} %get-tuple-element.25), channel_id=1, source_target_pairs={{0,6},{1,7},{2,4},{3,5},{4,2},{5,3},{6,0},{7,1},{8,14},{9,15},{10,... | collective-permute-start | bytes 393224 | tf_op jit(solution)/shard_map/ppermute | solution.py:154
  24.7 6.4 %collective-permute-start.7 = (bf16[4,2,64,256]{3,2,1,0:T(8,128)(2,1)S(1)}, bf16[4,2,64,256]{3,2,1,0:T(8,128)(2,1)S(1)}, u32[]{:S(2)}, u32[]{:S(2)}) collective-permute-start(bf16[4,2,64,256]{3,2,1,0:T(8,128)(2,1)S(1)} %get-tuple-element.68), channel_id=1, source_target_pairs={{0,16},{1,17},{2,18},{3,19},{4,20},{5,21},{6,22},{7,23},{8,24},{9,... | collective-permute-start | bytes 786440 | tf_op jit(solution)/shard_map/ppermute | solution.py:154
  26.3 8.4 %collective-permute-start.3 = (bf16[4,2,64,256]{3,2,1,0:T(8,128)(2,1)S(1)}, bf16[4,2,64,256]{3,2,1,0:T(8,128)(2,1)S(1)}, u32[]{:S(2)}, u32[]{:S(2)}) collective-permute-start(bf16[4,2,64,256]{3,2,1,0:T(8,128)(2,1)S(1)} %get-tuple-element.70), channel_id=1, source_target_pairs={{0,1},{1,0},{2,3},{3,2},{4,5},{5,4},{6,7},{7,6},{8,9},{9,8},{10,11... | collective-permute-start | bytes 786440 | tf_op jit(solution)/shard_map/ppermute | solution.py:154
  31.2 16.5 %collective-permute-start.8 = (bf16[2,4,2,64,256]{4,3,2,1,0:T(8,128)(2,1)S(1)}, bf16[2,4,2,64,256]{4,3,2,1,0:T(8,128)(2,1)S(1)}, u32[]{:S(2)}, u32[]{:S(2)}) collective-permute-start(bf16[2,4,2,64,256]{4,3,2,1,0:T(8,128)(2,1)S(1)} %pad_maximum_fusion.1.refs_4_), channel_id=1, source_target_pairs={{0,1},{1,0},{2,3},{3,2},{4,5},{5,4},{6,7},{7,6},{8,9},{9,8},{10,11... | collective-permute-start | bytes 1572872 | tf_op jit(solution)/shard_map/ppermute | solution.py:154
  34.8 12.9 %collective-permute-start.5 = (bf16[2,4,2,64,256]{4,3,2,1,0:T(8,128)(2,1)S(1)}, bf16[2,4,2,64,256]{4,3,2,1,0:T(8,128)(2,1)S(1)}, u32[]{:S(2)}, u32[]{:S(2)}) collective-permute-start(bf16[2,4,2,64,256]{4,3,2,1,0:T(8,128)(2,1)S(1)} %pad_maximum_fusion.refs_0_), channel_id=1, source_target_pairs={{0,16},{1,17},{2,18},{3,19},{4,20},{5,21},{6,22},{7,23},{8,24},{9,... | collective-permute-start | bytes 1572872 | tf_op jit(solution)/shard_map/ppermute | solution.py:154
  35.1 13.8 %collective-permute-start.4 = (bf16[2,4,2,64,256]{4,3,2,1,0:T(8,128)(2,1)S(1)}, bf16[2,4,2,64,256]{4,3,2,1,0:T(8,128)(2,1)S(1)}, u32[]{:S(2)}, u32[]{:S(2)}) collective-permute-start(bf16[2,4,2,64,256]{4,3,2,1,0:T(8,128)(2,1)S(1)} %pad_maximum_fusion.refs_0_), channel_id=1, source_target_pairs={{0,8},{1,9},{2,10},{3,11},{4,12},{5,13},{6,14},{7,15},{8,0},{9,1},... | collective-permute-start | bytes 1572872 | tf_op jit(solution)/shard_map/ppermute | solution.py:154
  35.1 13.8 %collective-permute-start.9 = (bf16[2,4,2,64,256]{4,3,2,1,0:T(8,128)(2,1)S(1)}, bf16[2,4,2,64,256]{4,3,2,1,0:T(8,128)(2,1)S(1)}, u32[]{:S(2)}, u32[]{:S(2)}) collective-permute-start(bf16[2,4,2,64,256]{4,3,2,1,0:T(8,128)(2,1)S(1)} %pad_maximum_fusion.1.refs_4_), channel_id=1, source_target_pairs={{0,8},{1,9},{2,10},{3,11},{4,12},{5,13},{6,14},{7,15},{8,0},{9,1},... | collective-permute-start | bytes 1572872 | tf_op jit(solution)/shard_map/ppermute | solution.py:154
  62.5 26.6 %collective-permute-start.11 = (f32[16,2,64,256]{3,2,1,0:T(8,128)}, f32[16,2,64,256]{3,2,1,0:T(8,128)}, u32[]{:S(2)}, u32[]{:S(2)}) collective-permute-start(f32[16,2,64,256]{3,2,1,0:T(8,128)} %get-tuple-element.27), channel_id=1, source_target_pairs={{0,8},{1,9},{2,10},{3,11},{4,12},{5,13},{6,14},{7,15},{8,0},{9,1},... | collective-permute-start | bytes 6291464 | tf_op jit(solution)/shard_map/ppermute | solution.py:154
  96.5 19.9 %collective-permute-start.16 = (f16[4,2,2,32,256]{4,3,1,2,0:T(8,128)(2,1)S(1)}, f16[4,2,2,32,256]{4,3,1,2,0:T(8,128)(2,1)S(1)}, u32[]{:S(2)}, u32[]{:S(2)}) collective-permute-start(f16[4,2,2,32,256]{4,3,1,2,0:T(8,128)(2,1)S(1)} %bitcast.125), channel_id=1, source_target_pairs={{0,1},{1,0},{2,3},{3,2},{4,5},{5,4},{6,7},{7,6},{8,9},{9,8},{10,11... | collective-permute-start | bytes 786440 | tf_op jit(solution)/shard_map/ppermute | solution.py:154
  109.6 10.9 %collective-permute-start.15 = (f16[8,2,1,32,256]{4,3,2,1,0:T(8,128)(2,1)S(1)}, f16[8,2,1,32,256]{4,3,2,1,0:T(8,128)(2,1)S(1)}, u32[]{:S(2)}, u32[]{:S(2)}) collective-permute-start(f16[8,2,1,32,256]{4,3,2,1,0:T(8,128)(2,1)S(1)} %constant_dynamic-slice_fusion.14), channel_id=1, source_target_pairs={{0,16},{1,17},{2,18},{3,19},{4,20},{5,21},{6,22},{7,23},{8,24},{9,... | collective-permute-start | bytes 786440 | tf_op jit(solution)/shard_map/ppermute | solution.py:154
  113.6 12.6 %collective-permute-start.14 = (f16[4,2,2,32,256]{4,3,1,2,0:T(8,128)(2,1)S(1)}, f16[4,2,2,32,256]{4,3,1,2,0:T(8,128)(2,1)S(1)}, u32[]{:S(2)}, u32[]{:S(2)}) collective-permute-start(f16[4,2,2,32,256]{4,3,1,2,0:T(8,128)(2,1)S(1)} %bitcast.124), channel_id=1, source_target_pairs={{0,1},{1,0},{2,3},{3,2},{4,5},{5,4},{6,7},{7,6},{8,9},{9,8},{10,11... | collective-permute-start | bytes 786440 | tf_op jit(solution)/shard_map/ppermute | solution.py:154
  115.7 10.4 %collective-permute-start.13 = (f16[8,2,1,32,256]{4,3,2,1,0:T(8,128)(2,1)S(1)}, f16[8,2,1,32,256]{4,3,2,1,0:T(8,128)(2,1)S(1)}, u32[]{:S(2)}, u32[]{:S(2)}) collective-permute-start(f16[8,2,1,32,256]{4,3,2,1,0:T(8,128)(2,1)S(1)} %constant_dynamic-slice_fusion.17), channel_id=1, source_target_pairs={{0,16},{1,17},{2,18},{3,19},{4,20},{5,21},{6,22},{7,23},{8,24},{9,... | collective-permute-start | bytes 786440 | tf_op jit(solution)/shard_map/ppermute | solution.py:154
  120.6 10.0 %collective-permute-start.20 = (f16[4,2,1,32,256]{4,3,1,2,0:T(8,128)(2,1)S(1)}, f16[4,2,1,32,256]{4,3,1,2,0:T(8,128)(2,1)S(1)}, u32[]{:S(2)}, u32[]{:S(2)}) collective-permute-start(f16[4,2,1,32,256]{4,3,1,2,0:T(8,128)(2,1)S(1)} %constant_dynamic-slice_fusion.10), channel_id=1, source_target_pairs={{0,16},{1,17},{2,18},{3,19},{4,20},{5,21},{6,22},{7,23},{8,24},{9,... | collective-permute-start | bytes 393224 | tf_op jit(solution)/shard_map/ppermute | solution.py:154
  122.8 7.9 %collective-permute-start.19 = (f16[4,2,1,32,256]{4,3,1,2,0:T(8,128)(2,1)S(1)}, f16[4,2,1,32,256]{4,3,1,2,0:T(8,128)(2,1)S(1)}, u32[]{:S(2)}, u32[]{:S(2)}) collective-permute-start(f16[4,2,1,32,256]{4,3,1,2,0:T(8,128)(2,1)S(1)} %dynamic-slice_bitcast_fusion), channel_id=1, source_target_pairs={{0,1},{1,0},{2,3},{3,2},{4,5},{5,4},{6,7},{7,6},{8,9},{9,8},{10,11... | collective-permute-start | bytes 393224 | tf_op jit(solution)/shard_map/ppermute | solution.py:154
  126.3 9.0 %collective-permute-start.18 = (f16[4,2,1,32,256]{4,3,1,2,0:T(8,128)(2,1)S(1)}, f16[4,2,1,32,256]{4,3,1,2,0:T(8,128)(2,1)S(1)}, u32[]{:S(2)}, u32[]{:S(2)}) collective-permute-start(f16[4,2,1,32,256]{4,3,1,2,0:T(8,128)(2,1)S(1)} %constant_dynamic-slice_fusion.11), channel_id=1, source_target_pairs={{0,16},{1,17},{2,18},{3,19},{4,20},{5,21},{6,22},{7,23},{8,24},{9,... | collective-permute-start | bytes 393224 | tf_op jit(solution)/shard_map/ppermute | solution.py:154
  128.5 6.9 %collective-permute-start.17 = (f16[4,2,1,32,256]{4,3,1,2,0:T(8,128)(2,1)S(1)}, f16[4,2,1,32,256]{4,3,1,2,0:T(8,128)(2,1)S(1)}, u32[]{:S(2)}, u32[]{:S(2)}) collective-permute-start(f16[4,2,1,32,256]{4,3,1,2,0:T(8,128)(2,1)S(1)} %dynamic-slice_bitcast_fusion.1), channel_id=1, source_target_pairs={{0,1},{1,0},{2,3},{3,2},{4,5},{5,4},{6,7},{7,6},{8,9},{9,8},{10,11... | collective-permute-start | bytes 393224 | tf_op jit(solution)/shard_map/ppermute | solution.py:154
  130.9 9.1 %collective-permute-start.25 = (f16[2,64,256]{2,1,0:T(8,128)(2,1)S(1)}, f16[2,64,256]{2,1,0:T(8,128)(2,1)S(1)}, u32[]{:S(2)}, u32[]{:S(2)}) collective-permute-start(f16[2,64,256]{2,1,0:T(8,128)(2,1)S(1)} %get-tuple-element.63), channel_id=1, source_target_pairs={{0,4},{1,5},{2,6},{3,7},{4,0},{5,1},{6,2},{7,3},{8,12},{9,13},{10,... | collective-permute-start | bytes 196616 | tf_op jit(solution)/shard_map/ppermute | solution.py:154
  131.0 9.0 %collective-permute-start.26 = (f16[2,64,256]{2,1,0:T(8,128)(2,1)S(1)}, f16[2,64,256]{2,1,0:T(8,128)(2,1)S(1)}, u32[]{:S(2)}, u32[]{:S(2)}) collective-permute-start(f16[2,64,256]{2,1,0:T(8,128)(2,1)S(1)} %get-tuple-element.62), channel_id=1, source_target_pairs={{0,6},{1,7},{2,4},{3,5},{4,2},{5,3},{6,0},{7,1},{8,14},{9,15},{10,... | collective-permute-start | bytes 196616 | tf_op jit(solution)/shard_map/ppermute | solution.py:154
  135.6 7.6 %collective-permute-start.22 = (f16[2,64,256]{2,1,0:T(8,128)(2,1)S(1)}, f16[2,64,256]{2,1,0:T(8,128)(2,1)S(1)}, u32[]{:S(2)}, u32[]{:S(2)}) collective-permute-start(f16[2,64,256]{2,1,0:T(8,128)(2,1)S(1)} %get-tuple-element.66), channel_id=1, source_target_pairs={{0,4},{1,5},{2,6},{3,7},{4,0},{5,1},{6,2},{7,3},{8,12},{9,13},{10,... | collective-permute-start | bytes 196616 | tf_op jit(solution)/shard_map/ppermute | solution.py:154
  136.9 6.3 %collective-permute-start.23 = (f16[2,64,256]{2,1,0:T(8,128)(2,1)S(1)}, f16[2,64,256]{2,1,0:T(8,128)(2,1)S(1)}, u32[]{:S(2)}, u32[]{:S(2)}) collective-permute-start(f16[2,64,256]{2,1,0:T(8,128)(2,1)S(1)} %get-tuple-element.65), channel_id=1, source_target_pairs={{0,6},{1,7},{2,4},{3,5},{4,2},{5,3},{6,0},{7,1},{8,14},{9,15},{10,... | collective-permute-start | bytes 196616 | tf_op jit(solution)/shard_map/ppermute | solution.py:154
  143.6 7.1 %collective-permute-start.28 = (f16[64,128]{1,0:T(8,128)(2,1)S(1)}, f16[64,128]{1,0:T(8,128)(2,1)S(1)}, u32[]{:S(2)}, u32[]{:S(2)}) collective-permute-start(f16[64,128]{1,0:T(8,128)(2,1)S(1)} %get-tuple-element.93), channel_id=1, source_target_pairs={{0,16},{1,17},{2,18},{3,19},{4,20},{5,21},{6,22},{7,23},{8,24},{9,... | collective-permute-start | bytes 49160 | tf_op jit(solution)/shard_map/ppermute | solution.py:154
  144.0 6.6 %collective-permute-start.29 = (f16[64,128]{1,0:T(8,128)(2,1)S(1)}, f16[64,128]{1,0:T(8,128)(2,1)S(1)}, u32[]{:S(2)}, u32[]{:S(2)}) collective-permute-start(f16[64,128]{1,0:T(8,128)(2,1)S(1)} %get-tuple-element.92), channel_id=1, source_target_pairs={{0,24},{1,25},{2,26},{3,27},{4,28},{5,29},{6,30},{7,31},{8,16},{9,... | collective-permute-start | bytes 49160 | tf_op jit(solution)/shard_map/ppermute | solution.py:154
  145.9 8.7 %collective-permute-start.37 = (f16[2,64,256]{2,1,0:T(8,128)(2,1)S(1)}, f16[2,64,256]{2,1,0:T(8,128)(2,1)S(1)}, u32[]{:S(2)}, u32[]{:S(2)}) collective-permute-start(f16[2,64,256]{2,1,0:T(8,128)(2,1)S(1)} %reshape.151), channel_id=1, source_target_pairs={{0,2},{1,3},{2,0},{3,1},{4,6},{5,7},{6,4},{7,5},{8,10},{9,11},{10,... | collective-permute-start | bytes 196616 | tf_op jit(solution)/shard_map/ppermute | solution.py:154
  147.3 8.4 %collective-permute-start.38 = (f16[2,64,256]{2,1,0:T(8,128)(2,1)S(1)}, f16[2,64,256]{2,1,0:T(8,128)(2,1)S(1)}, u32[]{:S(2)}, u32[]{:S(2)}) collective-permute-start(f16[2,64,256]{2,1,0:T(8,128)(2,1)S(1)} %reshape.151), channel_id=1, source_target_pairs={{0,4},{1,5},{2,6},{3,7},{4,0},{5,1},{6,2},{7,3},{8,12},{9,13},{10,... | collective-permute-start | bytes 196616 | tf_op jit(solution)/shard_map/ppermute | solution.py:154
  149.6 6.9 %collective-permute-start.39 = (f16[2,64,256]{2,1,0:T(8,128)(2,1)S(1)}, f16[2,64,256]{2,1,0:T(8,128)(2,1)S(1)}, u32[]{:S(2)}, u32[]{:S(2)}) collective-permute-start(f16[2,64,256]{2,1,0:T(8,128)(2,1)S(1)} %reshape.151), channel_id=1, source_target_pairs={{0,6},{1,7},{2,4},{3,5},{4,2},{5,3},{6,0},{7,1},{8,14},{9,15},{10,... | collective-permute-start | bytes 196616 | tf_op jit(solution)/shard_map/ppermute | solution.py:154
  151.6 9.6 %collective-permute-start.31 = (f16[2,64,256]{2,1,0:T(8,128)(2,1)S(1)}, f16[2,64,256]{2,1,0:T(8,128)(2,1)S(1)}, u32[]{:S(2)}, u32[]{:S(2)}) collective-permute-start(f16[2,64,256]{2,1,0:T(8,128)(2,1)S(1)} %reshape.147), channel_id=1, source_target_pairs={{0,4},{1,5},{2,6},{3,7},{4,0},{5,1},{6,2},{7,3},{8,12},{9,13},{10,... | collective-permute-start | bytes 196616 | tf_op jit(solution)/shard_map/ppermute | solution.py:154
  154.6 6.6 %collective-permute-start.32 = (f16[2,64,256]{2,1,0:T(8,128)(2,1)S(1)}, f16[2,64,256]{2,1,0:T(8,128)(2,1)S(1)}, u32[]{:S(2)}, u32[]{:S(2)}) collective-permute-start(f16[2,64,256]{2,1,0:T(8,128)(2,1)S(1)} %reshape.147), channel_id=1, source_target_pairs={{0,6},{1,7},{2,4},{3,5},{4,2},{5,3},{6,0},{7,1},{8,14},{9,15},{10,... | collective-permute-start | bytes 196616 | tf_op jit(solution)/shard_map/ppermute | solution.py:154
  156.6 7.1 %collective-permute-start.40 = (f16[4,2,64,256]{3,2,1,0:T(8,128)(2,1)S(1)}, f16[4,2,64,256]{3,2,1,0:T(8,128)(2,1)S(1)}, u32[]{:S(2)}, u32[]{:S(2)}) collective-permute-start(f16[4,2,64,256]{3,2,1,0:T(8,128)(2,1)S(1)} %get-tuple-element.58), channel_id=1, source_target_pairs={{0,1},{1,0},{2,3},{3,2},{4,5},{5,4},{6,7},{7,6},{8,9},{9,8},{10,11... | collective-permute-start | bytes 786440 | tf_op jit(solution)/shard_map/ppermute | solution.py:154
  161.3 7.3 %collective-permute-start.33 = (f16[4,2,64,256]{3,2,1,0:T(8,128)(2,1)S(1)}, f16[4,2,64,256]{3,2,1,0:T(8,128)(2,1)S(1)}, u32[]{:S(2)}, u32[]{:S(2)}) collective-permute-start(f16[4,2,64,256]{3,2,1,0:T(8,128)(2,1)S(1)} %get-tuple-element.60), channel_id=1, source_target_pairs={{0,1},{1,0},{2,3},{3,2},{4,5},{5,4},{6,7},{7,6},{8,9},{9,8},{10,11... | collective-permute-start | bytes 786440 | tf_op jit(solution)/shard_map/ppermute | solution.py:154
  (24 other events, 176.6 us)
Sparse Core Ops, SparseCore 0:
  10.4 66.1 all-gather.2
